TPU v7x, 256 devices: a whole 4x4x8 slice. The times are simulated.
256 devices in a mesh: tok: 32 (over x, z_lo, core), exp: 8 (over z_hi, y).
Axes of the slice: x: 4, y: 4, z: 8 (z_hi: 2, z_lo: 4; z = z_hi * 4 + z_lo), core: 2. Of those that a mesh axis runs over, the one named last changes fastest.
Arguments:
- tokens: bfloat16 [24576, 4096], P('tok'), may hold values from -6 to 6
- route_ids: int32 [24576, 8], P('tok'), may hold values from 0 to 127, all different within a row; in each aligned block of 768 rows (0 to 767, 768 to 1535, ...) at most 128 rows name the same one
- whiten: bfloat16 [16, 4096, 4096], P('exp', 'tok'), may hold values from -0.09375 to 0.09375
- deltas: bfloat16 [16, 4096, 1536], P('exp', 'tok'), may hold values from -6 to 6
- basis: bfloat16 [4096, 768], P('exp'), may hold values from -0.09375 to 0.09375
Outputs:
- gram: float32 [4096, 1, 4096], P('tok', None, 'exp')
- coefficients: float32 [768, 16, 1536], P('tok', 'exp')
- basis_gram: float32 [768, 768], P('tok')
Inputs may be any that keep to these rules, and one draw needn't show every extreme that they name: `route_ids`: each row names 8 different experts; among the rows of one device (aligned blocks of 768 rows) no expert is named by more than 128 rows.
All inputs are finite; a program needn't handle non-finite values.
Results may differ from a plain program's by a relative error of at most 0.0029.
Values may be sent and summed in bfloat16 or wider, within the bound.
A program may use at most 128 MiB of HBM per device.

v0:
```python
import jax
import jax.numpy as jnp
from jax import lax
from jax.sharding import Mesh
from jax.sharding import PartitionSpec as P

H = 1536
NROUTE = 128
TOP = 8
GRAM_EXP = 1
CAP = 128
TOK = ("tok_0", "tok_1", "tok_2")


def split_up(x, dim, count):
    before, after = (x.shape[:dim], x.shape[dim + 1 :])
    return jnp.moveaxis(x.reshape(*before, count, -1, *after), dim, 0)


def joined_along(pieces, dim):
    lengths = list(pieces.shape[1:])
    lengths[dim] *= pieces.shape[0]
    return jnp.moveaxis(pieces, 0, dim).reshape(lengths)


def turned_blocks(pieces, axes, turns):
    inside = pieces.shape[1:]
    filled = pieces.reshape(*(lax.axis_size(a) for a in axes), *inside)
    for k in turns:
        filled = lax.all_to_all(filled, axes[k], k, k, tiled=True)
    return filled.reshape(-1, *inside)


def two_step_exchange(x, groups, turns, split_dim, concat_dim):
    count = lax.axis_size(groups[0]) * lax.axis_size(groups[1])
    pieces = split_up(x, split_dim, count)
    return joined_along(turned_blocks(pieces, groups, turns), concat_dim)


def scatter_pairs(x, chips, core, dim):
    sizes = (lax.axis_size(chips), lax.axis_size(core))
    pieces = split_up(x, dim, sizes[0] * sizes[1])
    inside = pieces.shape[1:]
    pieces = pieces.reshape(*sizes, *inside).swapaxes(0, 1).reshape(-1, *inside)
    pieces = lax.psum_scatter(pieces, core, scatter_dimension=0, tiled=True)
    return lax.psum_scatter(pieces, chips, scatter_dimension=0, tiled=True)[0]


def sent_to_all(x, axis):
    count = lax.axis_size(axis)
    return lax.all_to_all(jnp.broadcast_to(x[None], (count, *x.shape)), axis, 0, 0, tiled=True)


def of_everyone(x, axis):
    return sent_to_all(x, axis).sum(axis=0)


def shards(tokens, route_ids, whiten, deltas, basis):
    tok_count = lax.axis_size(TOK)
    exp_count = lax.axis_size("exp")
    tok_rows, width = tokens.shape
    col_width = width // exp_count
    col_start = lax.axis_index("exp") * col_width
    scale = NROUTE / (TOP * tok_rows * tok_count)
    expert_ids = jnp.arange(GRAM_EXP, dtype=jnp.int32)
    hits = jnp.any(route_ids[:, :, None] == expert_ids[None, None, :], axis=1)
    hit = hits.astype(jnp.bfloat16)
    order = jnp.argsort(1 - hits.T.astype(jnp.int32), axis=1, stable=True)[:, :CAP]
    slot_hit = jnp.take_along_axis(hit.T, order, axis=1)
    packed = tokens[order] * slot_hit[:, :, None]
    packed_cols = lax.dynamic_slice_in_dim(packed, col_start, col_width, 2)
    row_parts = two_step_exchange(packed, (("tok_0", "tok_1"), "tok_2"), (1, 0), 2, 1)
    gram = (
        jnp.einsum(
            "gtd,gtc->dgc",
            row_parts,
            lax.all_gather(packed_cols, TOK, axis=1, tiled=True),
            preferred_element_type=jnp.float32,
        )
        * scale
    )
    local_experts, factor_rows, _ = whiten.shape
    part = whiten
    whitened = jnp.einsum(
        "erc,ck->erk",
        part,
        lax.all_gather(basis, "exp", axis=0, tiled=True),
        preferred_element_type=jnp.float32,
    ).astype(jnp.bfloat16)
    part = whitened
    coefficients = scatter_pairs(
        jnp.einsum("erk,erh->keh", part, deltas, preferred_element_type=jnp.float32),
        ("tok_0", "tok_1"),
        "tok_2",
        0,
    )
    products = jnp.einsum(
        "keh,leh->kl",
        coefficients,
        lax.all_gather(coefficients, TOK, axis=0, tiled=True),
        precision=lax.Precision.HIGHEST,
        preferred_element_type=jnp.float32,
    )
    basis_gram = of_everyone(products, "exp") / (local_experts * exp_count * H)
    return (gram, coefficients, basis_gram)


def solution(mesh):
    torus = Mesh(
        mesh.devices.reshape(4, 4, 2, mesh.shape["exp"]), ("tok_0", "tok_1", "tok_2", "exp")
    )
    placed = (P(TOK, None), P(TOK, None), P("exp", TOK, None), P("exp", TOK, None), P("exp", None))
    return jax.shard_map(
        shards,
        mesh=torus,
        in_specs=placed,
        out_specs=(P(TOK, None, "exp"), P(TOK, "exp", None), P(TOK, None)),
        check_vma=False,
    )
```

profile of v0, /device:TPU:1, one launch (start us, length us, event | category | flops | bytes accessed | tf_op | source)
XLA Modules:
  0.0 487.6 jit_solution(12351287060595633826)
XLA Ops:
  8.0 0.0 copy-start
  8.0 0.0 all-gather.7.cloned.1.call-start
  8.1 0.7 all-gather.7.cloned.1.call-update
  8.7 0.0 reduce-scatter.3.cloned.1.call-start
  8.8 146.2 %all-gather.7.cloned.1.call-done = bf16[4096,768]{1,0:T(8,128)(2,1)} async-done(((bf16[512,768]{1,0:T(8,128)(2,1)}), bf16[4096,768]{1,0:T(8,128)(2,1)}) %all-gather.7.cloned.1.call-update) | async-done | bytes 6291472 | tf_op jit(solution)/shard_map/all_gather | solution.py:87
  155.0 0.0 copy-done
  155.0 10.8 %fusion.10 = f32[2,768,1536]{2,1,0:T(8,128)} fusion(bf16[2,128,1536]{2,1,0:T(8,128)(2,1)} %param.8, bf16[2,128,4096]{2,1,0:T(8,128)(2,1)S(1)} %copy-done, bf16[4096,768]{1,0:T(8,128)(2,1)} %all-gather.7.cloned.1.call-done), kind=kOutput, calls=%fused_computation.9 | convolution fusion | flops 2214789120 | bytes 18612224 | tf_op jit(solution)/shard_map/erk,erh->keh/dot_general | solution.py:92
  165.8 8.6 %copy.31 = f32[2,16,24,2,1536]{4,2,3,1,0:T(8,128)} copy(f32[2,16,24,2,1536]{4,2,0,1,3:T(8,128)} %bitcast.53) | data formatting | bytes 18874368 | tf_op jit(solution)/shard_map/transpose | solution.py:44
  174.4 0.0 reduce-scatter.3.cloned.1.call-update
  174.4 0.0 reduce-scatter.5.cloned.1.call-start
  174.4 18.8 %reduce-scatter.3.cloned.1.call-done = f32[16,24,2,1536]{3,1,2,0:T(8,128)} async-done(((f32[32,24,2,1536]{3,1,2,0:T(8,128)}), f32[16,24,2,1536]{3,1,2,0:T(8,128)}) %reduce-scatter.3.cloned.1.call-update) | async-done | bytes 4718608 | tf_op jit(solution)/shard_map/reduce_scatter | solution.py:45
  193.3 0.0 reduce-scatter.5.cloned.1.call-update
  193.3 0.0 sort.19.cloned.1.call-start
  193.4 0.0 copy-done.2
  193.4 0.6 sub.19
  194.0 0.6 iota.7
  194.6 0.0 sort.19.cloned.1.call-update
  194.6 0.0 all-gather.9.cloned.1.call-start
  194.6 114.5 %reduce-scatter.5.cloned.1.call-done = f32[1,24,2,1536]{3,1,2,0:T(8,128)} async-done(((f32[16,24,2,1536]{3,1,2,0:T(8,128)}), f32[1,24,2,1536]{3,1,2,0:T(8,128)}) %reduce-scatter.5.cloned.1.call-update) | async-done | bytes 294928 | tf_op jit(solution)/shard_map/reduce_scatter | solution.py:46
  309.2 0.0 all-gather.9.cloned.1.call-update
  309.2 0.0 all-gather.5.cloned.1.call-start
  309.3 0.0 sort.19.cloned.1.call-done
  309.3 0.6 fusion.23
  309.9 1.3 gather_fusion.1
  311.2 5.8 %gather_fusion = bf16[128,4096]{1,0:T(8,128)(2,1)S(1)} fusion(bf16[768,4096]{1,0:T(8,128)(2,1)} %param.5, s32[1024]{0:T(1024)S(1)} %pad_clamp_fusion), kind=kCustom, calls=%fused_computation | custom fusion | bytes 2097664 | tf_op jit(solution)/shard_map/gather | solution.py:70
  317.0 0.6 fusion.21
  317.6 0.7 dynamic-slice_multiply_fusion
  318.3 0.0 all-gather.5.cloned.1.call-update
  318.3 0.0 copy-start.1
  318.4 0.2 copy.35
  318.6 0.4 copy_multiply_fusion
  319.0 0.1 copy.28
  319.1 5.2 %all_to_all.15 = bf16[16,2,1,128,128]{4,3,0,2,1:T(8,128)(2,1)S(1)} all-to-all(bf16[16,2,1,128,128]{4,3,0,2,1:T(8,128)(2,1)S(1)} %copy.28), channel_id=1, replica_groups=mesh['tok_0'=4,'tok_1'=4,'tok_2'=2,'exp'=8] {'tok_2'}, dimensions={1} | all-to-all | bytes 2097152 | tf_op jit(solution)/shard_map/all_to_all | solution.py:30
  324.3 1.1 copy.29
  325.3 3.8 all-to-all-start.1
  329.2 70.6 %all-gather.9.cloned.1.call-done = f32[1,768,2,1536]{3,1,2,0:T(8,128)} async-done(((f32[1,24,2,1536]{3,1,2,0:T(8,128)}), f32[1,768,2,1536]{3,1,2,0:T(8,128)}) %all-gather.9.cloned.1.call-update) | async-done | bytes 9437200 | tf_op jit(solution)/shard_map/all_gather | solution.py:100
  399.8 0.0 copy-done.1
  399.8 10.1 %fusion.18 = f32[24,768]{1,0:T(8,128)S(1)} fusion(f32[1,768,2,1536]{3,1,2,0:T(8,128)} %all-gather.9.cloned.1.call-done, f32[1,24,2,1536]{3,1,2,0:T(8,128)S(1)} %copy-done.1), kind=kOutput, calls=%fused_computation.12 | convolution fusion | flops 679477248 | bytes 9805824 | tf_op jit(solution)/shard_map/keh,leh->kl/dot_general | solution.py:97
  409.9 0.0 all-to-all-done.1
  409.9 0.9 broadcast_in_dim.19
  410.8 7.7 %all-to-all-start.2 = ((f32[8,24,768]{2,1,0:T(8,128)}), f32[8,24,768]{2,1,0:T(8,128)}, u32[]{:S(2)}, u32[]{:S(2)}) async-start(f32[8,24,768]{2,1,0:T(8,128)} %broadcast_in_dim.19), calls=%async_computation.4 | async-start | bytes 1179648 | tf_op jit(solution)/shard_map/all_to_all | solution.py:51
  418.5 53.2 %all-gather.5.cloned.1.call-done = bf16[1,4096,512]{2,1,0:T(8,128)(2,1)} async-done(((bf16[1,128,512]{2,1,0:T(8,128)(2,1)}), bf16[1,4096,512]{2,1,0:T(8,128)(2,1)}) %all-gather.5.cloned.1.call-update) | async-done | bytes 4194320 | tf_op jit(solution)/shard_map/all_gather | solution.py:77
  471.8 4.2 fusion.15
  476.0 1.8 copy.32
  477.7 0.9 copy.33
  478.7 0.0 all-to-all-done.2
  478.7 1.1 reduce_sum.9
  479.8 0.6 broadcast_multiply_fusion
  (5 shorter events, 0.0 us)
Async XLA Ops:
  8.0 147.0 %copy-start = (bf16[2,128,4096]{2,1,0:T(8,128)(2,1)S(1)}, bf16[2,128,4096]{2,1,0:T(8,128)(2,1)}, u32[]{:S(2)}) copy-start(bf16[2,128,4096]{2,1,0:T(8,128)(2,1)} %param.7) | copy-start | bytes 6291460
  8.0 147.0 %all-gather.7.cloned.1.call-start = ((), (), s32[]{:S(2)}) async-start(), calls=%async_computation.6 | async-start | bytes 7077888 | tf_op jit(solution)/shard_map/all_gather | solution.py:87
  8.7 184.5 %reduce-scatter.3.cloned.1.call-start = ((), (), s32[]{:S(2)}) async-start(), calls=%async_computation.7 | async-start | bytes 14155776 | tf_op jit(solution)/shard_map/reduce_scatter | solution.py:45
  174.4 19.0 %copy-start.2 = (s32[768,8]{0,1:T(8,128)S(1)}, s32[768,8]{0,1:T(8,128)}, u32[]{:S(2)}) copy-start(s32[768,8]{0,1:T(8,128)} %param.6) | copy-start | bytes 73732
  174.4 134.8 %reduce-scatter.5.cloned.1.call-start = ((), (), s32[]{:S(2)}) async-start(), calls=%async_computation.8 | async-start | bytes 5013504 | tf_op jit(solution)/shard_map/reduce_scatter | solution.py:46
  193.3 116.0 %sort.19.cloned.1.call-start = ((), (), s32[]{:S(2)}) async-start(), calls=%async_computation.10 | async-start | bytes 18464 | tf_op jit(solution)/shard_map/jit(argsort)/sort | solution.py:68
  194.6 205.2 %all-gather.9.cloned.1.call-start = ((), (), s32[]{:S(2)}) async-start(), calls=%async_computation.9 | async-start | bytes 9732096 | tf_op jit(solution)/shard_map/all_gather | solution.py:100
  309.2 162.6 %all-gather.5.cloned.1.call-start = ((), (), s32[]{:S(2)}) async-start(), calls=%async_computation.5 | async-start | bytes 4325376 | tf_op jit(solution)/shard_map/all_gather | solution.py:77
  318.3 81.5 %copy-start.1 = (f32[1,24,2,1536]{3,1,2,0:T(8,128)S(1)}, f32[1,24,2,1536]{3,1,2,0:T(8,128)}, u32[]{:S(2)}) copy-start(f32[1,24,2,1536]{3,1,2,0:T(8,128)} %reduce-scatter.5.cloned.1.call-done) | copy-start | bytes 884740
  325.3 84.6 %all-to-all-start.1 = ((bf16[16,2,1,128,128]{4,3,1,2,0:T(8,128)(2,1)}), bf16[16,2,1,128,128]{4,3,1,2,0:T(8,128)(2,1)S(1)}, u32[]{:S(2)}, u32[]{:S(2)}) async-start(bf16[16,2,1,128,128]{4,3,1,2,0:T(8,128)(2,1)} %copy.29), calls=%async_computation.1 | async-start | bytes 2097152 | tf_op jit(solution)/shard_map/all_to_all | solution.py:30
  410.8 67.9 %all-to-all-start.2 = ((f32[8,24,768]{2,1,0:T(8,128)}), f32[8,24,768]{2,1,0:T(8,128)}, u32[]{:S(2)}, u32[]{:S(2)}) async-start(f32[8,24,768]{2,1,0:T(8,128)} %broadcast_in_dim.19), calls=%async_computation.4 | async-start | bytes 1179648 | tf_op jit(solution)/shard_map/all_to_all | solution.py:51
Sparse Core Ops, SparseCore 0:
  11.8 143.1 all-gather.6
  174.5 18.7 reduce-scatter.2
  196.0 113.0 reduce-scatter.4
  311.0 88.7 all-gather.8
  402.2 69.5 all-gather.4
Sparse Core Ops, SparseCore 1:
  196.8 2.5 sort.21.cloned.1.call-done
  (1 shorter events, 0.0 us)
where the time goes:
time: 488 us
  waiting for transfers between devices  404 us (83%)
  matrix products  25.1 us (5%)
  local copies, waits for them, and re-layouts  21.9 us (4%)
  between operations  15.3 us (3%)
  starting transfers between devices  11.8 us (2%)
  blocking collectives  5.15 us (1%)
    all_gather x1, waiting for transfers between devices, shards(): lax.all_gather(basis, 'exp', axis=0, tiled=True)  146 us
    reduce_scatter x1, waiting for transfers between devices, scatter_pairs(): return lax.psum_scatter(pieces, chips, scatter_dimension=0, tiled=True)[0]  115 us
    all_gather x1, waiting for transfers between devices, shards(): lax.all_gather(coefficients, TOK, axis=0, tiled=True)  70.6 us
    all_gather x1, waiting for transfers between devices, shards(): lax.all_gather(packed_cols, TOK, axis=1, tiled=True)  53.2 us
    reduce_scatter x1, waiting for transfers between devices, scatter_pairs(): pieces = lax.psum_scatter(pieces, core, scatter_dimension=0, tiled=True)  18.8 us
    dot_general x1, matrix products, shards(): jnp.einsum('erk,erh->keh', part, deltas, preferred_element_type=jnp.float32)  10.8 us
    dot_general x1, matrix products, shards(): jnp.einsum('keh,leh->kl', coefficients, lax.all_gather(coefficients, TOK,...  10.1 us
  transfers between devices with their start and end apart: 7, of which 5 were waited for; matrix products, arithmetic and copies ran while one was open for 6% of the time, Pallas kernels for 0%

commit v1 on v0

v1 whole, which is shorter than its diff:
```python
import jax
import jax.numpy as jnp
from jax import lax
from jax.experimental import pallas as pl
from jax.experimental.pallas import tpu as pltpu
from jax.sharding import Mesh
from jax.sharding import PartitionSpec as P

H = 1536
NROUTE = 128
TOP = 8
GRAM_EXP = 1
CAP = 128
EXPERTS = 16
TOK = ("x", "w", "c")
EXP = ("h", "y")
MESH = pl.DeviceIdType.MESH
F32 = jnp.float32
BF16 = jnp.bfloat16


class Ids:
    def __init__(self, **counts):
        self.total = 0
        for name, count in counts.items():
            setattr(self, name, self.total)
            self.total += count


S = Ids(
    loc=4, ya=4, fa=1, fb=1, yfa=4, yfb=4, wh=2, dx=4, dc=4, wx=4, tz=4, sc=1, co=16, e1=4, e2=4, e3=4, e4=1
)


def mm(a, b):
    return lax.dot_general(a, b, (((1,), (0,)), ((), ())), preferred_element_type=F32)


def mm_t(a, b):
    return lax.dot_general(a, b, (((0,), (0,)), ((), ())), preferred_element_type=F32)


def kernel(
    whiten, deltas, basis, coef_out, gram_out,
    bb, ww, dg, wg, ws, acc, tsum, ts, rz, spad, xs, st, cg, gs, er1, e2s, er2, er3, q4, er4, send, recv,
):
    x, w, c = lax.axis_index("x"), lax.axis_index("w"), lax.axis_index("c")
    h, y = lax.axis_index("h"), lax.axis_index("y")
    me, far = h * 4 + y, (1 - h) * 4 + y
    z = h * 4 + w
    up, down = lax.rem(z + 1, 8), lax.rem(z + 7, 8)
    half = pl.ds(pl.multiple_of(c * 384, 128), 384)

    def around(i, d):
        return lax.rem(i + d, 4)

    def remote(src, dst, s, r, dev):
        return pltpu.make_async_remote_copy(
            src_ref=src, dst_ref=dst, send_sem=send.at[s], recv_sem=recv.at[r], device_id=dev, device_id_type=MESH
        )

    def at_x(i):
        return (i, w, c, h, y)

    def at_w(i):
        return (x, i, c, h, y)

    def at_y(i):
        return (x, w, c, h, i)

    def at_z(i):
        return (x, lax.rem(i, 4), c, i // 4, y)

    other = (x, w, 1 - c, h, y)
    up_dev, down_dev = at_z(up), at_z(down)

    near_a, near_b = jnp.where(w == 0, me, far), jnp.where(w == 3, me, far)
    low, high = pl.ds(0, 256), pl.ds(256, 256)
    send_a = remote(bb.at[near_a, low], bb.at[near_a, low], S.fa, S.fa, down_dev)
    send_b = remote(bb.at[near_b, high], bb.at[near_b, high], S.fb, S.fb, up_dev)
    first_a = remote(basis.at[low, half], bb.at[me, low], S.fa, S.fa, down_dev)
    first_b = remote(basis.at[high, half], bb.at[me, high], S.fb, S.fb, up_dev)

    @pl.when(w == 0)
    def _():
        first_a.start()

    @pl.when(w == 3)
    def _():
        first_b.start()

    own_y = [remote(basis.at[:, half], bb.at[me], S.ya + d, S.ya + d, at_y(around(y, d))) for d in (1, 2, 3)]
    for copy in own_y:
        copy.start()
    mine = pl.multiple_of(c * 128, 128)
    wh = [remote(whiten.at[e], ww.at[pl.ds(e * 256 + mine, 128)], S.wh + e, S.wh + e, other) for e in (0, 1)]
    loc = [pltpu.make_async_copy(whiten.at[e], ww.at[pl.ds(e * 256 + mine, 128)], recv.at[S.loc + e]) for e in (0, 1)]
    loc.append(pltpu.make_async_copy(basis.at[:, half], bb.at[me], recv.at[S.loc + 2]))
    for copy in loc + wh:
        copy.start()

    def delta_part(i):
        return deltas.at[i // 2, :, pl.ds(pl.multiple_of(lax.rem(i, 2) * 768, 128), 768)]

    loc.append(pltpu.make_async_copy(delta_part(x), dg.at[x, c], recv.at[S.loc + 3]))
    loc[-1].start()
    dc = [remote(delta_part(x), dg.at[x, c], S.dc, S.dc, other)]
    dc[0].start()
    dx = [remote(delta_part(around(x, d)), dg.at[x, c], S.dx + d, S.dx + d, at_x(around(x, d))) for d in (1, 2, 3)]
    for copy in dx:
        copy.start()

    far_ya = [remote(bb.at[far, low], bb.at[far, low], S.yfa + d, S.yfa + d, at_y(around(y, d))) for d in (1, 2, 3)]
    far_yb = [remote(bb.at[far, high], bb.at[far, high], S.yfb + d, S.yfb + d, at_y(around(y, d))) for d in (1, 2, 3)]

    def take_a():
        send_a.wait_recv()

        @pl.when(w != 0)
        def _():
            send_a.start()

        for copy in far_ya:
            copy.start()

    def take_b():
        send_b.wait_recv()

        @pl.when(w != 3)
        def _():
            send_b.start()

        for copy in far_yb:
            copy.start()

    pl.when(w >= 2)(take_a)
    pl.when(w < 2)(take_b)

    for copy in loc[:3]:
        copy.wait()
    for copy in wh:
        copy.wait_recv()

    def add_block(block, first=False):
        part = mm(ww[:, pl.ds(pl.multiple_of(block * 512, 512), 512)], bb[block])
        acc[...] = part if first else acc[...] + part

    add_block(me, True)
    for d in (1, 2, 3):
        dx[d - 1].wait_recv()
        src = around(x, 4 - d)
        dc.append(remote(dg.at[src, c], dg.at[src, c], S.dc + d, S.dc + d, other))
        dc[-1].start()
    pl.when(w >= 2)(take_b)
    pl.when(w < 2)(take_a)

    for d in (1, 2, 3):
        own_y[d - 1].wait_recv()
        add_block(h * 4 + around(y, 4 - d))
    add_block(far)
    for d in (1, 2, 3):
        far_ya[d - 1].wait_recv()
        far_yb[d - 1].wait_recv()
        add_block((1 - h) * 4 + around(y, 4 - d))

    ws[...] = acc[...].astype(BF16)

    def expert_rows(i):
        return pl.ds(pl.multiple_of((i // 2) * 256, 256), 256)

    wx = [
        remote(ws.at[expert_rows(around(x, d))], wg.at[x], S.wx + d, S.wx + d, at_x(around(x, d))) for d in (1, 2, 3)
    ]
    for copy in wx:
        copy.start()
    loc[3].wait()
    for copy in dc:
        copy.wait_recv()

    def rows_of(i):
        return dg[i].reshape(256, 768)

    tsum[...] = mm_t(rows_of(x), ws[expert_rows(x)])
    for d in (1, 2, 3):
        wx[d - 1].wait_recv()
        src = around(x, 4 - d)
        tsum[...] += mm_t(rows_of(src), wg[src])

    ts[...] = tsum[...].astype(BF16).reshape(4, 192, 384)
    tz = [remote(ts.at[around(w, d)], rz.at[w], S.tz + d, S.tz + d, at_w(around(w, d))) for d in (2, 1, 3)]
    for copy in tz:
        copy.start()
    spad[...] = jnp.zeros_like(spad)
    total = tsum[pl.ds(pl.multiple_of(w * 192, 64), 192), :]
    for copy, d in zip(tz, (2, 1, 3)):
        copy.wait_recv()
        total += rz[around(w, 4 - d)].astype(F32)
    spad[pl.ds(pl.multiple_of(lax.rem(w, 2) * 64, 64), 192), :] = total
    xs[c] = total.astype(BF16)
    swap = remote(xs.at[c], xs.at[c], S.sc, S.sc, other)
    swap.start()
    st[...] = spad[...].T.reshape(16, 24, 256)

    def piece_dev(p):
        return (2 * c + p // 8, lax.rem(p, 8) // 2, lax.rem(p, 2), h, y)

    def is_me(dev):
        return (dev[0] == x) & (dev[1] == w) & (dev[2] == c)

    from_me = x * 4 + w

    def piece(p):
        return remote(st.at[p], cg.at[from_me], S.co + p, S.co + from_me, piece_dev(p))

    @pl.loop(0, 16)
    def _(p):
        here = is_me(piece_dev(p))

        @pl.when(here)
        def _():
            pltpu.make_async_copy(st.at[p], cg.at[from_me], recv.at[S.co + from_me]).start()

        @pl.when(jnp.logical_not(here))
        def _():
            piece(p).start()

    left = xs[c]
    swap.wait_recv()
    gram = jnp.concatenate([mm_t(left, xs[0]), mm_t(left, xs[1])], axis=1)
    for p in range(16):
        gs[p // 8, p % 2, (p % 8) // 2, 0:24, :] = gram[24 * p : 24 * p + 24].astype(BF16)

    def sum_dev(j, k):
        return (2 * c + j, w, k, h, y)

    e1 = {(j, k): remote(gs.at[j, k], er1.at[x], S.e1 + 2 * j + k, S.e1 + x, sum_dev(j, k)) for j in (0, 1) for k in (0, 1)}
    for (j, k), copy in e1.items():
        here = is_me(sum_dev(j, k))

        @pl.when(here)
        def _():
            pltpu.make_async_copy(gs.at[j, k], er1.at[x], recv.at[S.e1 + x]).start()

        @pl.when(jnp.logical_not(here))
        def _():
            copy.start()

    for i in range(4):
        pltpu.make_async_copy(er1.at[i], er1.at[i], recv.at[S.e1 + i]).wait()
        part = er1[i, :, 0:24, :].astype(F32)
        e2s[...] = part if i == 0 else e2s[...] + part
    e2 = [remote(e2s.at[around(w, d)], er2.at[w], S.e2 + d, S.e2 + d, at_w(around(w, d))) for d in (2, 1, 3)]
    for copy in e2:
        copy.start()
    row = e2s[w]
    for copy, d in zip(e2, (2, 1, 3)):
        copy.wait_recv()
        row += er2[around(w, 4 - d)]
    er3[y] = row
    e3 = [remote(er3.at[y], er3.at[y], S.e3 + d, S.e3 + d, at_y(around(y, d))) for d in (2, 1, 3)]
    for copy in e3:
        copy.start()

    for i in range(16):
        pltpu.make_async_copy(cg.at[i], cg.at[i], recv.at[S.co + i]).wait()
    for i in range(4):
        for pair in (0, 1):
            even, odd = cg[4 * i + 2 * pair], cg[4 * i + 2 * pair + 1]
            at = (i % 2) * 768 + pair * 384
            coef_out[i // 2, :, at : at + 128] = even[:, 0:128]
            coef_out[i // 2, :, at + 128 : at + 256] = even[:, 128:256] + odd[:, 0:128]
            coef_out[i // 2, :, at + 256 : at + 384] = odd[:, 128:256]

    for copy in e3:
        copy.wait_recv()
    q4[...] = (er3[0] + er3[1]) + (er3[2] + er3[3])
    e4 = remote(q4, er4, S.e4, S.e4, (x, w, c, 1 - h, y))
    e4.start()
    e4.wait_recv()
    gram_out[...] = (q4[...] + er4[...]) * (1.0 / (EXPERTS * H))

    for copy in own_y + wh + dc + dx + [send_a, send_b] + far_ya + far_yb + wx + tz + [swap] + e2 + e3 + [e4]:
        copy.wait_send()

    @pl.loop(0, 16)
    def _(p):
        @pl.when(jnp.logical_not(is_me(piece_dev(p))))
        def _():
            piece(p).wait_send()

    for (j, k), copy in e1.items():

        @pl.when(jnp.logical_not(is_me(sum_dev(j, k))))
        def _():
            copy.wait_send()


def coefficients_and_gram(whiten, deltas, basis):
    anywhere = pl.BlockSpec(memory_space=pl.ANY)
    vmem = pl.BlockSpec(memory_space=pltpu.VMEM)
    return pl.pallas_call(
        kernel,
        out_shape=(
            jax.ShapeDtypeStruct((2, 24, H), F32),
            jax.ShapeDtypeStruct((24, 768), F32),
        ),
        in_specs=[anywhere] * 3,
        out_specs=(vmem, vmem),
        scratch_shapes=[
            pltpu.VMEM((8, 512, 384), BF16),
            pltpu.VMEM((512, 4096), BF16),
            pltpu.VMEM((4, 2, 128, 768), BF16),
            pltpu.VMEM((4, 256, 384), BF16),
            pltpu.VMEM((512, 384), BF16),
            pltpu.VMEM((512, 384), F32),
            pltpu.VMEM((768, 384), F32),
            pltpu.VMEM((4, 192, 384), BF16),
            pltpu.VMEM((4, 192, 384), BF16),
            pltpu.VMEM((256, 384), F32),
            pltpu.VMEM((2, 192, 384), BF16),
            pltpu.VMEM((16, 24, 256), F32),
            pltpu.VMEM((16, 24, 256), F32),
            pltpu.VMEM((2, 2, 4, 32, 768), BF16),
            pltpu.VMEM((4, 4, 32, 768), BF16),
            pltpu.VMEM((4, 24, 768), F32),
            pltpu.VMEM((4, 24, 768), F32),
            pltpu.VMEM((4, 24, 768), F32),
            pltpu.VMEM((24, 768), F32),
            pltpu.VMEM((24, 768), F32),
            pltpu.SemaphoreType.DMA((S.total,)),
            pltpu.SemaphoreType.DMA((S.total,)),
        ],
        compiler_params=pltpu.CompilerParams(has_side_effects=True, vmem_limit_bytes=48 << 20),
        cost_estimate=pl.CostEstimate(flops=4 * 10**9, bytes_accessed=20 * 10**6, transcendentals=0),
    )(whiten, deltas, basis)


def split_up(x, dim, count):
    before, after = (x.shape[:dim], x.shape[dim + 1 :])
    return jnp.moveaxis(x.reshape(*before, count, -1, *after), dim, 0)


def joined_along(pieces, dim):
    lengths = list(pieces.shape[1:])
    lengths[dim] *= pieces.shape[0]
    return jnp.moveaxis(pieces, 0, dim).reshape(lengths)


def turned_blocks(pieces, axes, turns):
    inside = pieces.shape[1:]
    filled = pieces.reshape(*(lax.axis_size(a) for a in axes), *inside)
    for k in turns:
        filled = lax.all_to_all(filled, axes[k], k, k, tiled=True)
    return filled.reshape(-1, *inside)


def two_step_exchange(x, groups, turns, split_dim, concat_dim):
    count = lax.axis_size(groups[0]) * lax.axis_size(groups[1])
    pieces = split_up(x, split_dim, count)
    return joined_along(turned_blocks(pieces, groups, turns), concat_dim)


def routed_gram(tokens, route_ids):
    tok_count = lax.axis_size(TOK)
    exp_count = lax.axis_size(EXP)
    tok_rows, width = tokens.shape
    col_width = width // exp_count
    col_start = lax.axis_index(EXP) * col_width
    scale = NROUTE / (TOP * tok_rows * tok_count)
    expert_ids = jnp.arange(GRAM_EXP, dtype=jnp.int32)
    hits = jnp.any(route_ids[:, :, None] == expert_ids[None, None, :], axis=1)
    hit = hits.astype(jnp.bfloat16)
    order = jnp.argsort(1 - hits.T.astype(jnp.int32), axis=1, stable=True)[:, :CAP]
    slot_hit = jnp.take_along_axis(hit.T, order, axis=1)
    packed = tokens[order] * slot_hit[:, :, None]
    packed_cols = lax.dynamic_slice_in_dim(packed, col_start, col_width, 2)
    row_parts = two_step_exchange(packed, (("x", "w"), "c"), (1, 0), 2, 1)
    return (
        jnp.einsum(
            "gtd,gtc->dgc",
            row_parts,
            lax.all_gather(packed_cols, TOK, axis=1, tiled=True),
            preferred_element_type=jnp.float32,
        )
        * scale
    )


def shards(tokens, route_ids, whiten, deltas, basis):
    coefficients, basis_gram = coefficients_and_gram(whiten, deltas, basis)
    gram = routed_gram(tokens, route_ids)
    return gram, coefficients.transpose(1, 0, 2), basis_gram


def solution(mesh):
    torus = Mesh(mesh.devices.reshape(4, 4, 2, 2, 4), TOK + EXP)
    placed = (P(TOK, None), P(TOK, None), P(EXP, TOK, None), P(EXP, TOK, None), P(EXP, None))
    return jax.shard_map(
        shards,
        mesh=torus,
        in_specs=placed,
        out_specs=(P(TOK, None, EXP), P(TOK, EXP, None), P(TOK, None)),
        check_vma=False,
    )
```

time: 488 us -> 167 us (0.34)
  waiting for transfers between devices: 404 us -> 0.02 us
  Pallas kernels: 0 us -> 112 us
  matrix products: 25.1 us -> 3.77 us
  starting transfers between devices: 11.8 us -> 6.54 us
    all_gather x3 -> x1, waiting for transfers between devices: 270 us -> 0.01 us  [routed_gram(): lax.all_gather(packed_cols, TOK, axis=1, tiled=True)]
    reduce_scatter x2 -> x0, waiting for transfers between devices: 133 us -> none  [the longest x1 115 us: scatter_pairs(): return lax.psum_scatter(pieces, chips, scatter_dimension=0, tiled=True)[0]]
    pallas_call x0 -> x1, Pallas kernels: none -> 112 us  [coefficients_and_gram(): pl.pallas_call(kernel, out_shape=(jax.ShapeDtypeStruct((2, 24, H), F32),...]
    dot_general x3 -> x1, matrix products: 25.1 us -> 3.77 us  [routed_gram(): jnp.einsum('gtd,gtc->dgc', row_parts, lax.all_gather(packed_cols, TOK, ax...]
    transpose x1 -> x0, local copies, waits for them, and re-layouts: 8.58 us -> none  [scatter_pairs(): pieces = pieces.reshape(*sizes, *inside).swapaxes(0, 1).reshape(-1, *inside)]
    all_to_all x1 -> x0, starting transfers between devices: 7.73 us -> none  [sent_to_all(): lax.all_to_all(jnp.broadcast_to(x[None], (count, *x.shape)), axis, 0, 0,...]
  transfers between devices with their start and end apart: 7 -> 2, of which waited for: 5 -> 0; matrix products, arithmetic and copies ran while one was open for 6% -> 2% of each run, Pallas kernels for 0% -> 68%
where the time goes in v1:
time: 167 us; the launch traced here: 166 us
  Pallas kernels  112 us (67%)
  local copies, waits for them, and re-layouts  17.9 us (11%)
  between operations  14.2 us (9%)
  blocking collectives  7.57 us (5%)
  starting transfers between devices  6.54 us (4%)
  matrix products  3.77 us (2%)
  other arithmetic  3.32 us (2%)
    pallas_call x1, Pallas kernels, coefficients_and_gram(): pl.pallas_call(kernel, out_shape=(jax.ShapeDtypeStruct((2, 24, H), F32),...  112 us
    all_to_all x1, blocking collectives, turned_blocks(): filled = lax.all_to_all(filled, axes[k], k, k, tiled=True)  7.57 us
    all_to_all x1, starting transfers between devices, turned_blocks(): filled = lax.all_to_all(filled, axes[k], k, k, tiled=True)  6.5 us
    gather x1, local copies, waits for them, and re-layouts, routed_gram(): packed = tokens[order] * slot_hit[:, :, None]  5.8 us
    sort x2, local copies, waits for them, and re-layouts, routed_gram(): jnp.argsort(1 - hits.T.astype(jnp.int32), axis=1, stable=True)[:, :CAP]  4.69 us
    unnamed x11, local copies, waits for them, and re-layouts  3.81 us
    dot_general x1, matrix products, routed_gram(): jnp.einsum('gtd,gtc->dgc', row_parts, lax.all_gather(packed_cols, TOK, ax...  3.77 us
  transfers between devices with their start and end apart: 2, of which 0 were waited for; matrix products, arithmetic and copies ran while one was open for 2% of the time, Pallas kernels for 68%

profile of v1, /device:TPU:1, one launch (start us, length us, event | category | flops | bytes accessed | tf_op | source)
XLA Modules:
  0.0 165.7 jit_solution(204284570542705682)
XLA Ops:
  7.2 0.0 sort.19.cloned.1.call-start
  7.2 0.8 compare_reduce_fusion
  8.0 0.6 sub.19
  8.6 0.6 iota.7
  9.1 0.0 sort.19.cloned.1.call-update
  9.2 0.0 all-gather.2.cloned.1.call-start
  9.2 4.6 %sort.19.cloned.1.call-done = (s32[1,768]{1,0:T(1,128)}, s32[1,768]{1,0:T(1,128)}) async-done(((s32[1,768]{1,0:T(1,128)}, s32[1,768]{1,0:T(1,128)}), (s32[1,768]{1,0:T(1,128)}, s32[1,768]{1,0:T(1,128)})) %sort.19.cloned.1.call-update) | async-done | bytes 6160 | tf_op jit(solution)/shard_map/jit(argsort)/sort | solution.py:373
  13.9 0.7 fusion.9
  14.6 5.8 %gather_fusion = bf16[128,4096]{1,0:T(8,128)(2,1)S(1)} fusion(bf16[768,4096]{1,0:T(8,128)(2,1)} %param.5, s32[1024]{0:T(1024)S(1)} %pad_clamp_fusion), kind=kCustom, calls=%fused_computation | custom fusion | bytes 2097664 | tf_op jit(solution)/shard_map/gather | solution.py:375
  20.4 1.3 gather_fusion.1
  21.6 0.7 fusion.8
  22.3 0.7 dynamic-slice_multiply_fusion
  23.1 0.0 all-gather.2.cloned.1.call-update
  23.1 0.2 copy.21
  23.4 0.4 copy_multiply_fusion
  23.8 0.0 copy-start
  23.8 0.0 copy-start.1
  23.8 0.1 copy.17
  23.9 7.6 %all_to_all.10 = bf16[16,2,1,128,128]{4,3,0,2,1:T(8,128)(2,1)S(1)} all-to-all(bf16[16,2,1,128,128]{4,3,0,2,1:T(8,128)(2,1)S(1)} %copy.17), channel_id=1, replica_groups=mesh['x'=4,'w'=4,'c'=2,'h'=2,'y'=4] {'c'}, dimensions={1} | all-to-all | bytes 2097152 | tf_op jit(solution)/shard_map/all_to_all | solution.py:353
  31.5 1.1 copy.18
  32.5 6.5 %all-to-all-start.1 = ((bf16[16,2,1,128,128]{4,3,1,2,0:T(8,128)(2,1)}), bf16[16,2,1,128,128]{4,3,1,2,0:T(8,128)(2,1)}, u32[]{:S(2)}, u32[]{:S(2)}) async-start(bf16[16,2,1,128,128]{4,3,1,2,0:T(8,128)(2,1)} %copy.18), calls=%async_computation.1 | async-start | bytes 2097152 | tf_op jit(solution)/shard_map/all_to_all | solution.py:353
  39.0 0.0 copy-done
  39.1 0.0 copy-done.1
  39.1 0.0 copy-start.2
  39.1 1.1 copy-done.2
  40.2 112.5 %shard_map.76 = (f32[2,24,1536]{2,1,0:T(8,128)S(1)}, f32[24,768]{1,0:T(8,128)S(1)}) custom-call(bf16[2,128,4096]{2,1,0:T(8,128)(2,1)S(1)} %copy-done, bf16[2,128,1536]{2,1,0:T(8,128)(2,1)S(1)} %copy-done.1, bf16[512,768]{1,0:T(8,128)(2,1)S(1)} %copy-done.2), custom_call_target="tpu_custom_call" | custom-call | flops 4000000000 | bytes 20000000 | tf_op jit(solution)/shard_map/pallas_call | solution.py:301
  152.7 0.9 copy.20
  153.6 0.0 all-to-all-done.1
  153.6 0.0 all-gather.2.cloned.1.call-done
  153.6 3.8 %fusion.5 = f32[128,1,512]{0,2,1:T(8,128)S(1)} fusion(bf16[4096,128]{1,0:T(8,128)(2,1)} %bitcast.7, bf16[1,4096,512]{2,1,0:T(8,128)(2,1)} %all-gather.2.cloned.1.call-done), kind=kOutput, calls=%fused_computation.5 | convolution fusion | flops 536936448 | bytes 5505024 | tf_op jit(solution)/shard_map/gtd,gtc->dgc/dot_general | solution.py:379
  157.4 0.8 copy.19
  158.2 0.6 copy.24
  (3 shorter events, 0.0 us)
Async XLA Ops:
  7.2 6.7 %sort.19.cloned.1.call-start = ((), (), s32[]{:S(2)}) async-start(), calls=%async_computation.3 | async-start | bytes 18464 | tf_op jit(solution)/shard_map/jit(argsort)/sort | solution.py:373
  9.2 144.5 %all-gather.2.cloned.1.call-start = ((), (), s32[]{:S(2)}) async-start(), calls=%async_computation.2 | async-start | bytes 4325376 | tf_op jit(solution)/shard_map/all_gather | solution.py:382
  23.8 15.3 %copy-start = (bf16[2,128,4096]{2,1,0:T(8,128)(2,1)S(1)}, bf16[2,128,4096]{2,1,0:T(8,128)(2,1)}, u32[]{:S(2)}) copy-start(bf16[2,128,4096]{2,1,0:T(8,128)(2,1)} %whiten.1) | copy-start | bytes 6291460
  23.8 15.3 %copy-start.1 = (bf16[2,128,1536]{2,1,0:T(8,128)(2,1)S(1)}, bf16[2,128,1536]{2,1,0:T(8,128)(2,1)}, u32[]{:S(2)}) copy-start(bf16[2,128,1536]{2,1,0:T(8,128)(2,1)} %deltas.1) | copy-start | bytes 2359300
  32.5 121.1 %all-to-all-start.1 = ((bf16[16,2,1,128,128]{4,3,1,2,0:T(8,128)(2,1)}), bf16[16,2,1,128,128]{4,3,1,2,0:T(8,128)(2,1)}, u32[]{:S(2)}, u32[]{:S(2)}) async-start(bf16[16,2,1,128,128]{4,3,1,2,0:T(8,128)(2,1)} %copy.18), calls=%async_computation.1 | async-start | bytes 2097152 | tf_op jit(solution)/shard_map/all_to_all | solution.py:353
  39.1 1.1 copy-start.2
Sparse Core Ops, SparseCore 0:
  11.0 2.6 sort.21.cloned.1.call-done
  23.2 84.8 all-gather.1
  (1 shorter events, 0.0 us)

commit v2 on v1

v2 whole, which is shorter than its diff:
```python
import jax
import jax.numpy as jnp
from jax import lax
from jax.experimental import pallas as pl
from jax.experimental.pallas import tpu as pltpu
from jax.sharding import Mesh
from jax.sharding import PartitionSpec as P

H = 1536
NROUTE = 128
TOP = 8
TOKENS = 24576
EXPERTS = 16
TOK = ("x", "w", "c")
EXP = ("h", "y")
MESH = pl.DeviceIdType.MESH
F32 = jnp.float32
BF16 = jnp.bfloat16


class Ids:
    def __init__(self, **counts):
        self.total = 0
        for name, count in counts.items():
            setattr(self, name, self.total)
            self.total += count


S = Ids(
    loc=16, fa=3, fb=3, yo=12, xo=12, yfa=12, yfb=12, wh=2, dx=4, dc=4, wx=12, tz=12, sc=3, co=16,
    e1=4, e2=4, e3=4, e4=1, gd=8, gc=4, gr=4, gy=4, gz=4,
)
PARTS = 3


def mm(a, b):
    return lax.dot_general(a, b, (((1,), (0,)), ((), ())), preferred_element_type=F32)


def mm_t(a, b):
    return lax.dot_general(a, b, (((0,), (0,)), ((), ())), preferred_element_type=F32)


def kernel(
    tokens, route_ids, whiten, deltas, basis, routed_out, coef_out, gram_out,
    tk, ids, pd, pc, gy, gc, gp, gx, gr,
    bb, xq, ww, dg, dt, wg, ws, acc, tsum, ts, rz, spad, xs, st, cg, gs, er1, e2s, e2b, er2, er3, q4, er4, send, recv,
):
    x, w, c = lax.axis_index("x"), lax.axis_index("w"), lax.axis_index("c")
    h, y = lax.axis_index("h"), lax.axis_index("y")
    me, far = h * 4 + y, (1 - h) * 4 + y
    z = h * 4 + w
    up, down = lax.rem(z + 1, 8), lax.rem(z + 7, 8)
    parts = range(PARTS)
    sent = []

    def around(i, d):
        return lax.rem(i + d, 4)

    def remote(src, dst, s, r, dev):
        return pltpu.make_async_remote_copy(
            src_ref=src, dst_ref=dst, send_sem=send.at[s], recv_sem=recv.at[r], device_id=dev, device_id_type=MESH
        )

    def start(copies):
        for copy in copies:
            copy.start()
        sent.extend(copies)
        return copies

    def arrive(copies):
        for copy in copies:
            copy.wait_recv()

    def local(src, dst, n):
        copy = pltpu.make_async_copy(src, dst, recv.at[S.loc + n])
        copy.start()
        return copy

    def at_x(i):
        return (i, w, c, h, y)

    def at_w(i):
        return (x, i, c, h, y)

    def at_y(i):
        return (x, w, c, h, i)

    def at_z(i):
        return (x, lax.rem(i, 4), c, i // 4, y)

    other = (x, w, 1 - c, h, y)
    up_dev, down_dev = at_z(up), at_z(down)
    opposite = (x, w, c, 1 - h, y)

    def columns(at, size):
        return pl.ds(pl.multiple_of(at, 128), size)

    mine = pl.multiple_of(c * 128, 128)
    basis_in = [local(basis.at[:, columns(c * 384 + 128 * n, 128)], bb.at[n, me], n) for n in parts]
    whiten_in = [local(whiten.at[e], ww.at[pl.ds(e * 256 + mine, 128)], 3 + e) for e in (0, 1)]
    ids_in = local(route_ids, ids, 5)

    def delta_part(i):
        return deltas.at[i // 2, :, columns(lax.rem(i, 2) * 768, 768)]

    delta_in = local(delta_part(x), dg.at[x, c], 6)
    token_in = [
        local(tokens.at[:, columns(1024 * i + 256 * y, 256)], tk.at[:, 256 * i : 256 * i + 256], 7 + i)
        for i in range(4)
    ]
    token_in.append(local(tokens.at[:, columns(512 * me, 512)], tk.at[:, 1024:1536], 11))

    barrier = pltpu.get_barrier_semaphore()
    friends = [(around(x, d), w, lax.rem(c + k, 2), h, y) for d in range(4) for k in (0, 1) if d or k]
    friends += [at_y(around(y, d)) for d in (1, 2, 3)] + [at_w(around(w, d)) for d in (1, 2, 3)] + [opposite]
    for dev in friends:
        pl.semaphore_signal(barrier, inc=1, device_id=dev, device_id_type=MESH)

    @pl.when(w == 0)
    def _():
        pl.semaphore_signal(barrier, inc=1, device_id=down_dev, device_id_type=MESH)

    @pl.when(w == 3)
    def _():
        pl.semaphore_signal(barrier, inc=1, device_id=up_dev, device_id_type=MESH)

    pl.semaphore_wait(barrier, len(friends) + jnp.where((w == 0) | (w == 3), 1, 0))

    near_a, near_b = jnp.where(w == 0, me, far), jnp.where(w == 3, me, far)
    low, high = pl.ds(0, 256), pl.ds(256, 256)
    send_a = [remote(bb.at[n, near_a, low], bb.at[n, near_a, low], S.fa + n, S.fa + n, down_dev) for n in parts]
    send_b = [remote(bb.at[n, near_b, high], bb.at[n, near_b, high], S.fb + n, S.fb + n, up_dev) for n in parts]
    for copy in basis_in:
        copy.wait()

    quarter = pl.ds(pl.multiple_of(x * 128, 128), 128)
    own_y = [
        [remote(bb.at[n, me, quarter], xq.at[n, x, d - 1], S.yo + 4 * n + d, S.yo + 4 * n + d, at_y(around(y, d))) for d in (1, 2, 3)]
        for n in parts
    ]
    own_x = [
        [remote(xq.at[n, x], xq.at[n, x], S.xo + 4 * n + d, S.xo + 4 * n + d, at_x(around(x, d))) for d in (1, 2, 3)]
        for n in parts
    ]
    for n in parts:

        @pl.when(w == 0)
        def _():
            send_a[n].start()

        @pl.when(w == 3)
        def _():
            send_b[n].start()

        start(own_y[n])

    wh = start([remote(whiten.at[e], ww.at[pl.ds(e * 256 + mine, 128)], S.wh + e, S.wh + e, other) for e in (0, 1)])
    dc = start([remote(delta_part(x), dg.at[x, c], S.dc, S.dc, other)])

    far_a = [
        [remote(bb.at[n, far, low], bb.at[n, far, low], S.yfa + 4 * n + d, S.yfa + 4 * n + d, at_y(around(y, d))) for d in (1, 2, 3)]
        for n in parts
    ]
    far_b = [
        [remote(bb.at[n, far, high], bb.at[n, far, high], S.yfb + 4 * n + d, S.yfb + 4 * n + d, at_y(around(y, d))) for d in (1, 2, 3)]
        for n in parts
    ]

    def take_a():
        for n in parts:
            send_a[n].wait_recv()

            @pl.when(w != 0)
            def _():
                send_a[n].start()

            for copy in far_a[n]:
                copy.start()

    def take_b():
        for n in parts:
            send_b[n].wait_recv()

            @pl.when(w != 3)
            def _():
                send_b[n].start()

            for copy in far_b[n]:
                copy.start()

    for n in parts:
        arrive(own_y[n])
        start(own_x[n])
        if n == 0:
            dx = start(
                [remote(delta_part(around(x, d)), dg.at[x, c], S.dx + d, S.dx + d, at_x(around(x, d))) for d in (1, 2, 3)]
            )
    pl.when(w >= 2)(take_a)
    pl.when(w < 2)(take_b)

    ids_in.wait()
    hit = jnp.max(jnp.where(ids[...] == 0, 1.0, 0.0), axis=0, keepdims=True)
    hits = jnp.broadcast_to(hit, (8, 768)).astype(BF16)
    earlier = lax.broadcasted_iota(jnp.int32, (768, 768), 0) <= lax.broadcasted_iota(jnp.int32, (768, 768), 1)
    place = mm(hits, jnp.where(earlier, 1.0, 0.0).astype(BF16))[0:1]
    place = jnp.broadcast_to(jnp.where(hit > 0.0, place, 0.0), (128, 768))
    slot = (lax.broadcasted_iota(jnp.int32, (128, 768), 0) + 1).astype(F32)
    pick = jnp.where(place == slot, 1.0, 0.0).astype(BF16)

    pl.when(w >= 2)(take_b)
    pl.when(w < 2)(take_a)
    sent.extend(send_a + send_b + sum(far_a, []) + sum(far_b, []))

    for copy in token_in:
        copy.wait()
    mine8 = 2 * x + c
    for n in range(4):
        part = mm(pick, tk[:, 256 * n : 256 * n + 256]).astype(BF16)
        pd[n, 0] = part[:, 0:128]
        pd[n, 1] = part[:, 128:256]
    pc[...] = mm(pick, tk[:, 1024:1536]).astype(BF16)
    gy[y, mine8] = pd[x, c]
    gc[mine8] = pc[...]

    delta_in.wait()
    for d in (1, 2, 3):
        dx[d - 1].wait_recv()
        src = around(x, 4 - d)
        dc += start([remote(dg.at[src, c], dg.at[src, c], S.dc + d, S.dc + d, other)])
    for copy in whiten_in:
        copy.wait()
    arrive(wh)
    arrive(dc)
    for i in range(4):
        dt[:, 256 * i : 256 * i + 256] = dg[i].reshape(256, 768).T

    def factor(block):
        return ww[:, columns(block * 512, 512)]

    def expert_rows(i):
        return pl.ds(pl.multiple_of((i // 2) * 256, 256), 256)

    def whitened(n):
        total = mm(factor(me), bb[n, me]) + mm(factor(far), bb[n, far])
        arrive(own_x[n])
        for d in (1, 2, 3):
            block = jnp.concatenate([xq[n, i, d - 1] for i in range(4)], axis=0)
            total += mm(factor(h * 4 + around(y, 4 - d)), block)
        for d in (1, 2, 3):
            from_y = (1 - h) * 4 + around(y, 4 - d)
            far_a[n][d - 1].wait_recv()
            far_b[n][d - 1].wait_recv()
            total += mm(factor(from_y), bb[n, from_y])
        ws[n] = total.astype(BF16)
        wg[n, x] = ws[n, expert_rows(x)]
        return start(
            [
                remote(ws.at[n, expert_rows(around(x, d))], wg.at[n, x], S.wx + 4 * n + d, S.wx + 4 * n + d, at_x(around(x, d)))
                for d in (1, 2, 3)
            ]
        )

    def hidden(n, wx):
        arrive(wx)
        tsum[n] = mm(dt[...], wg[n].reshape(1024, 128))
        ts[n] = tsum[n].astype(BF16).reshape(4, 192, 128)
        return start(
            [
                remote(ts.at[n, around(w, d)], rz.at[n, w], S.tz + 4 * n + d, S.tz + 4 * n + d, at_w(around(w, d)))
                for d in (2, 1, 3)
            ]
        )

    wx0 = whitened(0)
    wx1 = whitened(1)
    tz = [hidden(0, wx0)]
    wx2 = whitened(2)
    rows8 = start(
        [
            remote(
                pd.at[around(x, d), lax.rem(c + k, 2)], gy.at[y, mine8], S.gd + 2 * d + k, S.gd + 2 * d + k,
                (around(x, d), w, lax.rem(c + k, 2), h, y),
            )
            for d in range(4) for k in (0, 1) if d or k
        ]
    )
    cols = start([remote(pc, gc.at[mine8], S.gc + d, S.gc + d, at_x(around(x, d))) for d in (1, 2, 3)])
    cols_c = start([remote(pc, gc.at[mine8], S.gr, S.gr, other)])
    tz.append(hidden(1, wx1))
    tz.append(hidden(2, wx2))

    spad[...] = jnp.zeros_like(spad)
    swap = []
    for n in parts:
        total = tsum[n, pl.ds(pl.multiple_of(w * 192, 64), 192), :]
        for copy, d in zip(tz[n], (2, 1, 3)):
            copy.wait_recv()
            total += rz[n, around(w, 4 - d)].astype(F32)
        spad[pl.ds(pl.multiple_of(lax.rem(w, 2) * 64, 64), 192), 128 * n : 128 * n + 128] = total
        xs[c, n] = total.astype(BF16)
        swap += start([remote(xs.at[c, n], xs.at[c, n], S.sc + n, S.sc + n, other)])
    st[...] = spad[...].T.reshape(16, 24, 256)

    def piece_dev(p):
        return (2 * c + p // 8, lax.rem(p, 8) // 2, lax.rem(p, 2), h, y)

    def is_me(dev):
        return (dev[0] == x) & (dev[1] == w) & (dev[2] == c)

    from_me = x * 4 + w

    def piece(p):
        return remote(st.at[p], cg.at[from_me], S.co + p, S.co + from_me, piece_dev(p))

    @pl.loop(0, 16)
    def _(p):
        here = is_me(piece_dev(p))

        @pl.when(here)
        def _():
            pltpu.make_async_copy(st.at[p], cg.at[from_me], recv.at[S.co + from_me]).start()

        @pl.when(jnp.logical_not(here))
        def _():
            piece(p).start()

    arrive(swap)

    def wide(i):
        return jnp.concatenate([xs[i, n] for n in parts], axis=1)

    left = wide(c)
    for half in (0, 1):
        gram = mm_t(left, wide(half))
        for p in range(16):
            gs[p // 8, p % 2, (p % 8) // 2, :, 384 * half : 384 * half + 384] = gram[24 * p : 24 * p + 24].astype(BF16)

    def sum_dev(j, k):
        return (2 * c + j, w, k, h, y)

    e1 = {
        (j, k): remote(gs.at[j, k], er1.at[x], S.e1 + 2 * j + k, S.e1 + x, sum_dev(j, k)) for j in (0, 1) for k in (0, 1)
    }
    for (j, k), copy in e1.items():
        here = is_me(sum_dev(j, k))

        @pl.when(here)
        def _():
            pltpu.make_async_copy(gs.at[j, k], er1.at[x], recv.at[S.e1 + x]).start()

        @pl.when(jnp.logical_not(here))
        def _():
            copy.start()

    arrive(rows8)
    gy_all = start([remote(gy.at[y], gy.at[y], S.gy + d, S.gy + d, at_y(around(y, d))) for d in (1, 2, 3)])
    for d in (1, 2, 3):
        cols[d - 1].wait_recv()
        src = 2 * around(x, 4 - d) + c
        cols_c += start([remote(gc.at[src], gc.at[src], S.gr + d, S.gr + d, other)])

    for i in range(4):
        pltpu.make_async_copy(er1.at[i], er1.at[i], recv.at[S.e1 + i]).wait()
        part = er1[i].astype(F32)
        e2s[...] = part if i == 0 else e2s[...] + part
    e2b[...] = e2s[...].astype(BF16)
    e2 = start([remote(e2b.at[around(w, d)], er2.at[w], S.e2 + d, S.e2 + d, at_w(around(w, d))) for d in (2, 1, 3)])

    arrive(cols_c)
    arrive(gy_all)
    for i in range(4):
        gp[i] = mm_t(gy[i].reshape(1024, 128), gc[...].reshape(1024, 512))
    gx[...] = gp[...].astype(BF16)
    gz = start([remote(gx.at[around(w, d)], gr.at[w], S.gz + d, S.gz + d, at_w(around(w, d))) for d in (2, 1, 3)])

    row = e2s[w]
    for copy, d in zip(e2, (2, 1, 3)):
        copy.wait_recv()
        row += er2[around(w, 4 - d)].astype(F32)
    er3[y] = row
    e3 = start([remote(er3.at[y], er3.at[y], S.e3 + d, S.e3 + d, at_y(around(y, d))) for d in (2, 1, 3)])

    for i in range(16):
        pltpu.make_async_copy(cg.at[i], cg.at[i], recv.at[S.co + i]).wait()
    for i in range(4):
        for pair in (0, 1):
            even, odd = cg[4 * i + 2 * pair], cg[4 * i + 2 * pair + 1]
            at = (i % 2) * 768 + pair * 384
            coef_out[i // 2, :, at : at + 128] = even[:, 0:128]
            coef_out[i // 2, :, at + 128 : at + 256] = even[:, 128:256] + odd[:, 0:128]
            coef_out[i // 2, :, at + 256 : at + 384] = odd[:, 128:256]

    arrive(e3)
    q4[...] = (er3[0] + er3[1]) + (er3[2] + er3[3])
    e4 = start([remote(q4, er4, S.e4, S.e4, opposite)])
    routed = gp[w]
    for copy, d in zip(gz, (2, 1, 3)):
        copy.wait_recv()
        routed += gr[around(w, 4 - d)].astype(F32)
    routed_out[...] = routed * (NROUTE / (TOP * TOKENS))
    arrive(e4)
    gram_out[...] = (q4[...] + er4[...]) * (1.0 / (EXPERTS * H))

    for copy in sent:
        copy.wait_send()

    @pl.loop(0, 16)
    def _(p):
        @pl.when(jnp.logical_not(is_me(piece_dev(p))))
        def _():
            piece(p).wait_send()

    for (j, k), copy in e1.items():

        @pl.when(jnp.logical_not(is_me(sum_dev(j, k))))
        def _():
            copy.wait_send()


def whole(tokens, route_ids, whiten, deltas, basis):
    in_hbm = pl.BlockSpec(memory_space=pltpu.HBM)
    vmem = pl.BlockSpec(memory_space=pltpu.VMEM)
    return pl.pallas_call(
        kernel,
        out_shape=(
            jax.ShapeDtypeStruct((128, 512), F32),
            jax.ShapeDtypeStruct((2, 24, H), F32),
            jax.ShapeDtypeStruct((24, 768), F32),
        ),
        in_specs=[in_hbm] * 5,
        out_specs=(vmem, vmem, vmem),
        scratch_shapes=[
            pltpu.VMEM((768, 1536), BF16),
            pltpu.VMEM((8, 768), jnp.int32),
            pltpu.VMEM((4, 2, 128, 128), BF16),
            pltpu.VMEM((128, 512), BF16),
            pltpu.VMEM((4, 8, 128, 128), BF16),
            pltpu.VMEM((8, 128, 512), BF16),
            pltpu.VMEM((4, 128, 512), F32),
            pltpu.VMEM((4, 128, 512), BF16),
            pltpu.VMEM((4, 128, 512), BF16),
            pltpu.VMEM((PARTS, 8, 512, 128), BF16),
            pltpu.VMEM((PARTS, 4, 3, 128, 128), BF16),
            pltpu.VMEM((512, 4096), BF16),
            pltpu.VMEM((4, 2, 128, 768), BF16),
            pltpu.VMEM((768, 1024), BF16),
            pltpu.VMEM((PARTS, 4, 256, 128), BF16),
            pltpu.VMEM((PARTS, 512, 128), BF16),
            pltpu.VMEM((512, 128), F32),
            pltpu.VMEM((PARTS, 768, 128), F32),
            pltpu.VMEM((PARTS, 4, 192, 128), BF16),
            pltpu.VMEM((PARTS, 4, 192, 128), BF16),
            pltpu.VMEM((256, 384), F32),
            pltpu.VMEM((2, PARTS, 192, 128), BF16),
            pltpu.VMEM((16, 24, 256), F32),
            pltpu.VMEM((16, 24, 256), F32),
            pltpu.VMEM((2, 2, 4, 24, 768), BF16),
            pltpu.VMEM((4, 4, 24, 768), BF16),
            pltpu.VMEM((4, 24, 768), F32),
            pltpu.VMEM((4, 24, 768), BF16),
            pltpu.VMEM((4, 24, 768), BF16),
            pltpu.VMEM((4, 24, 768), F32),
            pltpu.VMEM((24, 768), F32),
            pltpu.VMEM((24, 768), F32),
            pltpu.SemaphoreType.DMA((S.total,)),
            pltpu.SemaphoreType.DMA((S.total,)),
        ],
        compiler_params=pltpu.CompilerParams(collective_id=0, has_side_effects=True, vmem_limit_bytes=52 << 20),
        cost_estimate=pl.CostEstimate(flops=4 * 10**9, bytes_accessed=20 * 10**6, transcendentals=0),
    )(tokens, route_ids, whiten, deltas, basis)


def shards(tokens, route_ids, whiten, deltas, basis):
    gram, coefficients, basis_gram = whole(tokens, route_ids.T, whiten, deltas, basis)
    return gram[:, None, :], coefficients.transpose(1, 0, 2), basis_gram


def solution(mesh):
    torus = Mesh(mesh.devices.reshape(4, 4, 2, 2, 4), TOK + EXP)
    placed = (P(TOK, None), P(TOK, None), P(EXP, TOK, None), P(EXP, TOK, None), P(EXP, None))
    return jax.shard_map(
        shards,
        mesh=torus,
        in_specs=placed,
        out_specs=(P(TOK, None, EXP), P(TOK, EXP, None), P(TOK, None)),
        check_vma=False,
    )
```

time: 167 us -> 98 us (0.59)
  the two profiles are of different devices: /device:TPU:1 before, /device:TPU:32 now
where the time goes in v2:
time: 98 us; the launch traced here: 97.8 us
  Pallas kernels  92.8 us (95%)
  local copies, waits for them, and re-layouts  4.41 us (4%)
    pallas_call x1, Pallas kernels, whole(): pl.pallas_call(kernel, out_shape=(jax.ShapeDtypeStruct((128, 512), F32),...  92.8 us
    unnamed x7, local copies, waits for them, and re-layouts  4.41 us

profile of v2, /device:TPU:32, one launch (start us, length us, event | category | flops | bytes accessed | tf_op | source)
XLA Modules:
  0.0 97.8 jit_solution(805157269823829661)
XLA Ops:
  0.6 0.0 copy-start
  0.6 1.1 %copy-done = bf16[2,128,1536]{2,1,0:T(8,128)(2,1)S(1)} copy-done((bf16[2,128,1536]{2,1,0:T(8,128)(2,1)S(1)}, bf16[2,128,1536]{2,1,0:T(8,128)(2,1)}, u32[]{:S(2)}) %copy-start) | copy-done | bytes 786456
  1.8 0.0 copy-start.1
  1.8 0.7 copy-done.1
  2.5 92.8 %shard_map.76 = (f32[128,512]{1,0:T(8,128)S(1)}, f32[2,24,1536]{2,1,0:T(8,128)S(1)}, f32[24,768]{1,0:T(8,128)S(1)}) custom-call(bf16[768,4096]{1,0:T(8,128)(2,1)} %tokens.1, s32[8,768]{1,0:T(8,128)S(1)} %bitcast.5, bf16[2,128,4096]{2,1,0:T(8,128)(2,1)} %whiten.1, bf16[2,128,1536]{2,1,0:T(8,128)(2,1)S(1)} %copy-done, bf16[512,768]{1,0:T(8,128)(2,1)} %basis.1), custom_call_target="tpu_custom_call" | custom-call | flops 4000000000 | bytes 20000000 | tf_op jit(solution)/shard_map/pallas_call | solution.py:424
  95.3 1.0 copy.8
  96.3 0.9 copy.9
  97.2 0.6 copy.11
Async XLA Ops:
  0.6 1.1 %copy-start = (bf16[2,128,1536]{2,1,0:T(8,128)(2,1)S(1)}, bf16[2,128,1536]{2,1,0:T(8,128)(2,1)}, u32[]{:S(2)}) copy-start(bf16[2,128,1536]{2,1,0:T(8,128)(2,1)} %deltas.1) | copy-start | bytes 2359300
  1.8 0.7 copy-start.1

commit v3 on v2

v3 whole, which is shorter than its diff:
```python
import jax
import jax.numpy as jnp
from jax import lax
from jax.experimental import pallas as pl
from jax.experimental.pallas import tpu as pltpu
from jax.sharding import Mesh
from jax.sharding import PartitionSpec as P

H = 1536
NROUTE = 128
TOP = 8
TOKENS = 24576
EXPERTS = 16
TOK = ("x", "w", "c")
EXP = ("h", "y")
MESH = pl.DeviceIdType.MESH
F32 = jnp.float32
BF16 = jnp.bfloat16


class Ids:
    def __init__(self, **counts):
        self.total = 0
        for name, count in counts.items():
            setattr(self, name, self.total)
            self.total += count


S = Ids(
    loc=16, zq=3, fx=12, yf=12, yo=12, xo=12, wh=2, dx=4, dc=4, wx=12, tz=12, sl=12, sr=8, co=16,
    e2=32, e3=8, gd=8, gc=4, gr=4, gy=4, gz=4,
)
PARTS = 3


def mm(a, b):
    return lax.dot_general(a, b, (((1,), (0,)), ((), ())), preferred_element_type=F32)


def mm_t(a, b):
    return lax.dot_general(a, b, (((0,), (0,)), ((), ())), preferred_element_type=F32)


def kernel(
    tokens, route_ids, whiten, deltas, basis, routed_out, coef_out, gram_out,
    tk, ids, pd, pc, gy, gc, gp, gx, gr,
    bb, xq, ww, dg, dt, wg, ws, acc, tsum, ts, rz, spad, sx, rx, g2, st, cg, e2b, er2, q4, er3, send, recv,
):
    x, w, c = lax.axis_index("x"), lax.axis_index("w"), lax.axis_index("c")
    h, y = lax.axis_index("h"), lax.axis_index("y")
    me, far = h * 4 + y, (1 - h) * 4 + y
    parts = range(PARTS)
    sent = []

    def around(i, d):
        return lax.rem(i + d, 4)

    def remote(src, dst, s, r, dev):
        return pltpu.make_async_remote_copy(
            src_ref=src, dst_ref=dst, send_sem=send.at[s], recv_sem=recv.at[r], device_id=dev, device_id_type=MESH
        )

    def start(copies):
        for copy in copies:
            copy.start()
        sent.extend(copies)
        return copies

    def arrive(copies):
        for copy in copies:
            copy.wait_recv()

    def local(src, dst, n):
        copy = pltpu.make_async_copy(src, dst, recv.at[S.loc + n])
        copy.start()
        return copy

    def at_x(i):
        return (i, w, c, h, y)

    def at_w(i):
        return (x, i, c, h, y)

    def at_y(i):
        return (x, w, c, h, i)

    other = (x, w, 1 - c, h, y)
    opposite = (x, w, c, 1 - h, y)

    def columns(at, size):
        return pl.ds(pl.multiple_of(at, 128), size)

    mine = pl.multiple_of(c * 128, 128)
    basis_in = [local(basis.at[:, columns(c * 384 + 128 * n, 128)], bb.at[n, me], n) for n in parts]
    whiten_in = [local(whiten.at[e], ww.at[pl.ds(e * 256 + mine, 128)], 3 + e) for e in (0, 1)]
    ids_in = local(route_ids, ids, 5)

    def delta_part(i):
        return deltas.at[i // 2, :, columns(lax.rem(i, 2) * 768, 768)]

    delta_in = local(delta_part(x), dg.at[x, c], 6)
    token_in = [
        local(tokens.at[:, columns(1024 * y, 1024)], tk.at[:, 0:1024], 7),
        local(tokens.at[:, columns(512 * me, 512)], tk.at[:, 1024:1536], 8),
    ]

    barrier = pltpu.get_barrier_semaphore()
    friends = [(around(x, d), w, lax.rem(c + k, 2), h, y) for d in range(4) for k in (0, 1) if d or k]
    friends += [at_y(around(y, d)) for d in (1, 2, 3)] + [at_w(around(w, d)) for d in (1, 2, 3)] + [opposite]
    for dev in friends:
        pl.semaphore_signal(barrier, inc=1, device_id=dev, device_id_type=MESH)

    ids_in.wait()
    hit = jnp.max(jnp.where(ids[...] == 0, 1.0, 0.0), axis=0, keepdims=True)
    hits = jnp.broadcast_to(hit, (8, 768)).astype(BF16)
    earlier = lax.broadcasted_iota(jnp.int32, (768, 768), 0) <= lax.broadcasted_iota(jnp.int32, (768, 768), 1)
    place = mm(hits, jnp.where(earlier, 1.0, 0.0).astype(BF16))[0:1]
    place = jnp.broadcast_to(jnp.where(hit > 0.0, place, 0.0), (128, 768))
    slot = (lax.broadcasted_iota(jnp.int32, (128, 768), 0) + 1).astype(F32)
    pick = jnp.where(place == slot, 1.0, 0.0).astype(BF16)

    for copy in token_in:
        copy.wait()
    mine8 = 2 * w + c
    for n in range(4):
        part = mm(pick, tk[:, 256 * n : 256 * n + 256]).astype(BF16)
        pd[n, 0] = part[:, 0:128]
        pd[n, 1] = part[:, 128:256]
    pc[...] = mm(pick, tk[:, 1024:1536]).astype(BF16)
    gy[y, mine8] = pd[w, c]
    gc[mine8] = pc[...]

    pl.semaphore_wait(barrier, len(friends))

    quarter = pl.ds(pl.multiple_of(x * 128, 128), 128)
    zq = [remote(bb.at[n, me, quarter], bb.at[n, me, quarter], S.zq + n, S.zq + n, opposite) for n in parts]
    fx = [
        [remote(bb.at[n, far, quarter], bb.at[n, far, quarter], S.fx + 4 * n + d, S.fx + 4 * n + d, at_x(around(x, d))) for d in (2, 1, 3)]
        for n in parts
    ]
    yf = [
        [remote(bb.at[n, far], bb.at[n, far], S.yf + 4 * n + d, S.yf + 4 * n + d, at_y(around(y, d))) for d in (2, 1, 3)]
        for n in parts
    ]
    own_y = [
        [
            remote(
                bb.at[n, me] if n == 0 else bb.at[n, me, quarter],
                bb.at[n, me] if n == 0 else xq.at[n, x, d - 1],
                S.yo + 4 * n + d, S.yo + 4 * n + d, at_y(around(y, d)),
            )
            for d in (1, 2, 3)
        ]
        for n in parts
    ]
    own_x = [
        [remote(xq.at[n, x], xq.at[n, x], S.xo + 4 * n + d, S.xo + 4 * n + d, at_x(around(x, d))) for d in (2, 1, 3)]
        for n in parts
    ]
    for n in parts:
        basis_in[n].wait()
        start([zq[n]])
    for n in parts:
        start(own_y[n])
    wh = start([remote(whiten.at[e], ww.at[pl.ds(e * 256 + mine, 128)], S.wh + e, S.wh + e, other) for e in (0, 1)])
    dc = start([remote(delta_part(x), dg.at[x, c], S.dc, S.dc, other)])

    def arrived(dst, sem):
        pltpu.make_async_copy(dst, dst, recv.at[sem]).wait()

    def factor(at, size):
        return ww[:, columns(at, size)]

    for n in parts:
        arrived(bb.at[n, far, quarter], S.zq + n)
        start(fx[n])
    dx = start([remote(delta_part(around(x, d)), dg.at[x, c], S.dx + d, S.dx + d, at_x(around(x, d))) for d in (2, 1, 3)])
    for copy in whiten_in:
        copy.wait()
    arrive(wh)
    acc[0] = mm(factor(me * 512, 512), bb[0, me])
    for n in parts:
        for d in (2, 1, 3):
            arrived(bb.at[n, far, quarter], S.fx + 4 * n + d)
        start(yf[n])
        if n:
            arrive(own_y[n])
            start(own_x[n])
    for n in (1, 2):
        acc[n] = mm(factor(me * 512, 512), bb[n, me])

    rows8 = start(
        [
            remote(
                pd.at[around(w, d), lax.rem(c + k, 2)], gy.at[y, mine8], S.gd + 2 * d + k, S.gd + 2 * d + k,
                (x, around(w, d), lax.rem(c + k, 2), h, y),
            )
            for d in range(4) for k in (0, 1) if d or k
        ]
    )
    cols = start([remote(pc, gc.at[mine8], S.gc + d, S.gc + d, at_w(around(w, d))) for d in (1, 2, 3)])
    cols_c = start([remote(pc, gc.at[mine8], S.gr, S.gr, other)])

    for n in parts:
        acc[n] += mm(factor(far * 512, 512), bb[n, far])

    for d in (1, 2, 3):
        block = h * 4 + around(y, 4 - d)
        arrived(bb.at[0, block], S.yo + d)
        acc[0] += mm(factor(block * 512, 512), bb[0, block])

    delta_in.wait()
    for copy, d in zip(dx, (2, 1, 3)):
        copy.wait_recv()
        src = around(x, 4 - d)
        dc += start([remote(dg.at[src, c], dg.at[src, c], S.dc + d, S.dc + d, other)])

    def from_y(d):
        return (1 - h) * 4 + around(y, 4 - d)

    def expert_rows(i):
        return pl.ds(pl.multiple_of((i // 2) * 256, 256), 256)

    def whitened(n):
        total = acc[n]
        if n:
            arrive(own_x[n])
            for d in (1, 2, 3):
                block = jnp.concatenate([xq[n, i, d - 1] for i in range(4)], axis=0)
                total += mm(factor((h * 4 + around(y, 4 - d)) * 512, 512), block)
        for d in (2, 1, 3):
            arrived(bb.at[n, from_y(d)], S.yf + 4 * n + d)
            total += mm(factor(from_y(d) * 512, 512), bb[n, from_y(d)])
        ws[n] = total.astype(BF16)
        wg[n, x] = ws[n, expert_rows(x)]
        return start(
            [
                remote(ws.at[n, expert_rows(around(x, d))], wg.at[n, x], S.wx + 4 * n + d, S.wx + 4 * n + d, at_x(around(x, d)))
                for d in (2, 1, 3)
            ]
        )

    def hidden(n, wx):
        arrive(wx)
        tsum[n] = mm(dt[...], wg[n].reshape(1024, 128))
        ts[n] = tsum[n].astype(BF16).reshape(4, 192, 128)
        return start(
            [
                remote(ts.at[n, around(w, d)], rz.at[n, w], S.tz + 4 * n + d, S.tz + 4 * n + d, at_w(around(w, d)))
                for d in (2, 1, 3)
            ]
        )

    wx0 = whitened(0)
    arrive(dc)
    for i in range(4):
        dt[:, 256 * i : 256 * i + 256] = dg[i].reshape(256, 768).T
    wx1 = whitened(1)
    tz = [hidden(0, wx0)]
    wx2 = whitened(2)
    tz.append(hidden(1, wx1))
    tz.append(hidden(2, wx2))

    arrive(rows8)
    gy_all = start([remote(gy.at[y], gy.at[y], S.gy + d, S.gy + d, at_y(around(y, d))) for d in (1, 2, 3)])
    for d in (1, 2, 3):
        cols[d - 1].wait_recv()
        src = 2 * around(w, 4 - d) + c
        cols_c += start([remote(gc.at[src], gc.at[src], S.gr + d, S.gr + d, other)])

    spad[...] = jnp.zeros_like(spad)
    swap, rows = [], {}
    for n in parts:
        total = tsum[n, pl.ds(pl.multiple_of(w * 192, 64), 192), :]
        for copy, d in zip(tz[n], (2, 1, 3)):
            copy.wait_recv()
            total += rz[n, around(w, 4 - d)].astype(F32)
        sx[n, x] = total.astype(BF16)
        swap.append(
            start([remote(sx.at[n, x], sx.at[n, x], S.sl + 4 * n + d, S.sl + 4 * n + d, at_x(around(x, d))) for d in (2, 1, 3)])
        )
        for j in (0, 1):
            if 0 <= n - j <= 1:
                start([remote(sx.at[n, x], rx.at[n - j, x], S.sr + 2 * n + j, S.sr + 4 * (n - j) + x, (2 * c + j, w, 1 - c, h, y))])
        spad[pl.ds(pl.multiple_of(lax.rem(w, 2) * 64, 64), 192), 128 * n : 128 * n + 128] = total
    st[...] = spad[...].T.reshape(16, 24, 256)

    def piece_dev(p):
        return (2 * c + p // 8, lax.rem(p, 8) // 2, lax.rem(p, 2), h, y)

    def is_me(dev):
        return (dev[0] == x) & (dev[1] == w) & (dev[2] == c)

    from_me = x * 4 + w

    def piece(p):
        return remote(st.at[p], cg.at[from_me], S.co + p, S.co + from_me, piece_dev(p))

    @pl.loop(0, 16)
    def _(p):
        here = is_me(piece_dev(p))

        @pl.when(here)
        def _():
            pltpu.make_async_copy(st.at[p], cg.at[from_me], recv.at[S.co + from_me]).start()

        @pl.when(jnp.logical_not(here))
        def _():
            piece(p).start()

    for n in parts:
        for d in (2, 1, 3):
            arrived(sx.at[n, around(x, 4 - d)], S.sl + 4 * n + d)
    odd = lax.rem(x, 2)

    @pl.when(c == x // 2)
    def _():
        rx[...] = sx[pl.ds(odd, 2)]

    @pl.when(c != x // 2)
    def _():
        for r in (0, 1):
            for i in range(4):
                arrived(rx.at[r, i], S.sr + 4 * r + i)

    lhs = jnp.concatenate([rx[r].reshape(768, 128) for r in (0, 1)], axis=1)
    g2[...] = mm_t(lhs, jnp.concatenate([sx[n].reshape(768, 128) for n in parts], axis=1))
    gram = g2[pl.ds(pl.multiple_of(odd * 64, 64), 192), :]
    for p in range(8):
        for n in parts:
            e2b[3 * p + n] = gram[24 * p : 24 * p + 24, 128 * n : 128 * n + 128].astype(BF16)

    def exp_dev(i, core, e):
        return (x, i, core, e // 4, lax.rem(e, 4))

    from_here = w * 8 + me

    def sum_piece(p):
        i, core, e = p // 6, lax.rem(p // 3, 2), 3 * c + lax.rem(p, 3)
        return (i == w) & (core == c) & (e == me), remote(
            e2b.at[p], er2.at[from_here], S.e2 + p, S.e2 + from_here, exp_dev(i, core, e)
        )

    @pl.loop(0, 24)
    def _(p):
        here, copy = sum_piece(p)

        @pl.when(here)
        def _():
            pltpu.make_async_copy(e2b.at[p], er2.at[from_here], recv.at[S.e2 + from_here]).start()

        @pl.when(jnp.logical_not(here))
        def _():
            copy.start()

    arrive(cols_c)
    arrive(gy_all)
    for i in range(4):
        gp[i] = mm_t(gy[i].reshape(1024, 128), gc[...].reshape(1024, 512))
    gx[...] = gp[...].astype(BF16)
    gz = start([remote(gx.at[around(x, d)], gr.at[x], S.gz + d, S.gz + d, at_x(around(x, d))) for d in (2, 1, 3)])

    e3 = [remote(q4, er3.at[me], S.e3 + d, S.e3 + me, exp_dev(w, c, lax.rem(me + d, 8))) for d in range(1, 8)]

    @pl.when(me < 6)
    def _():
        row = None
        for i in range(32):
            arrived(er2.at[i], S.e2 + i)
        for i in range(32):
            part = er2[i].astype(F32)
            row = part if i == 0 else row + part
        q4[...] = row * (1.0 / (EXPERTS * H))
        pltpu.make_async_copy(q4, er3.at[me], recv.at[S.e3 + me]).start()
        for copy in e3:
            copy.start()

    for i in range(16):
        pltpu.make_async_copy(cg.at[i], cg.at[i], recv.at[S.co + i]).wait()
    for i in range(4):
        for pair in (0, 1):
            even, odd = cg[4 * i + 2 * pair], cg[4 * i + 2 * pair + 1]
            at = (i % 2) * 768 + pair * 384
            coef_out[i // 2, :, at : at + 128] = even[:, 0:128]
            coef_out[i // 2, :, at + 128 : at + 256] = even[:, 128:256] + odd[:, 0:128]
            coef_out[i // 2, :, at + 256 : at + 384] = odd[:, 128:256]

    routed = gp[x]
    for copy, d in zip(gz, (2, 1, 3)):
        copy.wait_recv()
        routed += gr[around(x, 4 - d)].astype(F32)
    routed_out[...] = routed * (NROUTE / (TOP * TOKENS))

    for i in range(6):
        arrived(er3.at[i], S.e3 + i)
        gram_out[:, 128 * i : 128 * i + 128] = er3[i]

    for copy in sent:
        copy.wait_send()

    @pl.loop(0, 16)
    def _(p):
        @pl.when(jnp.logical_not(is_me(piece_dev(p))))
        def _():
            piece(p).wait_send()


    @pl.loop(0, 24)
    def _(p):
        here, copy = sum_piece(p)

        @pl.when(jnp.logical_not(here))
        def _():
            copy.wait_send()

    @pl.when(me < 6)
    def _():
        for copy in e3:
            copy.wait_send()


def whole(tokens, route_ids, whiten, deltas, basis):
    in_hbm = pl.BlockSpec(memory_space=pltpu.HBM)
    vmem = pl.BlockSpec(memory_space=pltpu.VMEM)
    return pl.pallas_call(
        kernel,
        out_shape=(
            jax.ShapeDtypeStruct((128, 512), F32),
            jax.ShapeDtypeStruct((2, 24, H), F32),
            jax.ShapeDtypeStruct((24, 768), F32),
        ),
        in_specs=[in_hbm] * 5,
        out_specs=(vmem, vmem, vmem),
        scratch_shapes=[
            pltpu.VMEM((768, 1536), BF16),
            pltpu.VMEM((8, 768), jnp.int32),
            pltpu.VMEM((4, 2, 128, 128), BF16),
            pltpu.VMEM((128, 512), BF16),
            pltpu.VMEM((4, 8, 128, 128), BF16),
            pltpu.VMEM((8, 128, 512), BF16),
            pltpu.VMEM((4, 128, 512), F32),
            pltpu.VMEM((4, 128, 512), BF16),
            pltpu.VMEM((4, 128, 512), BF16),
            pltpu.VMEM((PARTS, 8, 512, 128), BF16),
            pltpu.VMEM((PARTS, 4, 3, 128, 128), BF16),
            pltpu.VMEM((512, 4096), BF16),
            pltpu.VMEM((4, 2, 128, 768), BF16),
            pltpu.VMEM((768, 1024), BF16),
            pltpu.VMEM((PARTS, 4, 256, 128), BF16),
            pltpu.VMEM((PARTS, 512, 128), BF16),
            pltpu.VMEM((PARTS, 512, 128), F32),
            pltpu.VMEM((PARTS, 768, 128), F32),
            pltpu.VMEM((PARTS, 4, 192, 128), BF16),
            pltpu.VMEM((PARTS, 4, 192, 128), BF16),
            pltpu.VMEM((256, 384), F32),
            pltpu.VMEM((PARTS, 4, 192, 128), BF16),
            pltpu.VMEM((2, 4, 192, 128), BF16),
            pltpu.VMEM((256, 384), F32),
            pltpu.VMEM((16, 24, 256), F32),
            pltpu.VMEM((16, 24, 256), F32),
            pltpu.VMEM((24, 24, 128), BF16),
            pltpu.VMEM((32, 24, 128), BF16),
            pltpu.VMEM((24, 128), F32),
            pltpu.VMEM((6, 24, 128), F32),
            pltpu.SemaphoreType.DMA((S.total,)),
            pltpu.SemaphoreType.DMA((S.total,)),
        ],
        compiler_params=pltpu.CompilerParams(collective_id=0, has_side_effects=True, vmem_limit_bytes=52 << 20),
        cost_estimate=pl.CostEstimate(flops=4 * 10**9, bytes_accessed=20 * 10**6, transcendentals=0),
    )(*(pltpu.with_memory_space_constraint(a, pltpu.HBM) for a in (tokens, route_ids, whiten, deltas, basis)))


def shards(tokens, route_ids, whiten, deltas, basis):
    gram, coefficients, basis_gram = whole(tokens, route_ids.T, whiten, deltas, basis)
    return gram[:, None, :], coefficients.transpose(1, 0, 2), basis_gram


def solution(mesh):
    torus = Mesh(mesh.devices.reshape(4, 4, 2, 2, 4), TOK + EXP)
    placed = (P(TOK, None), P(TOK, None), P(EXP, TOK, None), P(EXP, TOK, None), P(EXP, None))
    return jax.shard_map(
        shards,
        mesh=torus,
        in_specs=placed,
        out_specs=(P(TOK, None, EXP), P(TOK, EXP, None), P(TOK, None)),
        check_vma=False,
    )
```

time: 98 us -> 87 us (0.89)
  the two profiles are of different devices: /device:TPU:32 before, /device:TPU:1 now
where the time goes in v3:
time: 87 us; the launch traced here: 86.7 us
  Pallas kernels  83.5 us (96%)
  local copies, waits for them, and re-layouts  2.55 us (3%)
    pallas_call x1, Pallas kernels, whole(): pl.pallas_call(kernel, out_shape=(jax.ShapeDtypeStruct((128, 512), F32),...  83.5 us
    unnamed x3, local copies, waits for them, and re-layouts  2.55 us

profile of v3, /device:TPU:1, one launch (start us, length us, event | category | flops | bytes accessed | tf_op | source)
XLA Modules:
  0.0 86.7 jit_solution(17240791238833316637)
XLA Ops:
  0.6 83.5 %shard_map.76 = (f32[128,512]{1,0:T(8,128)S(1)}, f32[2,24,1536]{2,1,0:T(8,128)S(1)}, f32[24,768]{1,0:T(8,128)S(1)}) custom-call(bf16[768,4096]{1,0:T(8,128)(2,1)} %tokens.1, s32[8,768]{1,0:T(8,128)} %bitcast.5, bf16[2,128,4096]{2,1,0:T(8,128)(2,1)} %whiten.1, bf16[2,128,1536]{2,1,0:T(8,128)(2,1)} %deltas.1, bf16[512,768]{1,0:T(8,128)(2,1)} %basis.1), custom_call_target="tpu_custom_call" | custom-call | flops 4000000000 | bytes 20000000 | tf_op jit(solution)/shard_map/pallas_call | solution.py:425
  84.2 1.0 %copy.8 = f32[128,1,512]{2,1,0:T(1,128)} copy(f32[128,1,512]{2,0,1:T(8,128)S(1)} %bitcast.4) | data formatting | bytes 524288
  85.1 0.9 %copy.9 = f32[24,2,1536]{2,1,0:T(2,128)} copy(f32[24,2,1536]{2,0,1:T(8,128)S(1)} %bitcast.3) | data formatting | bytes 589824
  86.1 0.6 copy.11

commit v4 on v3

--- a/solution.py
+++ b/solution.py
@@ -85,7 +85,7 @@
         return (x, w, c, h, i)
 
     other = (x, w, 1 - c, h, y)
-    opposite = (x, w, c, 1 - h, y)
+    opposite = (x, 3 - w, c, 1 - h, y)
 
     def columns(at, size):
         return pl.ds(pl.multiple_of(at, 128), size)
@@ -109,26 +109,6 @@
     friends += [at_y(around(y, d)) for d in (1, 2, 3)] + [at_w(around(w, d)) for d in (1, 2, 3)] + [opposite]
     for dev in friends:
         pl.semaphore_signal(barrier, inc=1, device_id=dev, device_id_type=MESH)
-
-    ids_in.wait()
-    hit = jnp.max(jnp.where(ids[...] == 0, 1.0, 0.0), axis=0, keepdims=True)
-    hits = jnp.broadcast_to(hit, (8, 768)).astype(BF16)
-    earlier = lax.broadcasted_iota(jnp.int32, (768, 768), 0) <= lax.broadcasted_iota(jnp.int32, (768, 768), 1)
-    place = mm(hits, jnp.where(earlier, 1.0, 0.0).astype(BF16))[0:1]
-    place = jnp.broadcast_to(jnp.where(hit > 0.0, place, 0.0), (128, 768))
-    slot = (lax.broadcasted_iota(jnp.int32, (128, 768), 0) + 1).astype(F32)
-    pick = jnp.where(place == slot, 1.0, 0.0).astype(BF16)
-
-    for copy in token_in:
-        copy.wait()
-    mine8 = 2 * w + c
-    for n in range(4):
-        part = mm(pick, tk[:, 256 * n : 256 * n + 256]).astype(BF16)
-        pd[n, 0] = part[:, 0:128]
-        pd[n, 1] = part[:, 128:256]
-    pc[...] = mm(pick, tk[:, 1024:1536]).astype(BF16)
-    gy[y, mine8] = pd[w, c]
-    gc[mine8] = pc[...]
 
     pl.semaphore_wait(barrier, len(friends))
 
@@ -165,6 +145,15 @@
     wh = start([remote(whiten.at[e], ww.at[pl.ds(e * 256 + mine, 128)], S.wh + e, S.wh + e, other) for e in (0, 1)])
     dc = start([remote(delta_part(x), dg.at[x, c], S.dc, S.dc, other)])
 
+    ids_in.wait()
+    hit = jnp.max(jnp.where(ids[...] == 0, 1.0, 0.0), axis=0, keepdims=True)
+    hits = jnp.broadcast_to(hit, (8, 768)).astype(BF16)
+    earlier = lax.broadcasted_iota(jnp.int32, (768, 768), 0) <= lax.broadcasted_iota(jnp.int32, (768, 768), 1)
+    place = mm(hits, jnp.where(earlier, 1.0, 0.0).astype(BF16))[0:1]
+    place = jnp.broadcast_to(jnp.where(hit > 0.0, place, 0.0), (128, 768))
+    slot = (lax.broadcasted_iota(jnp.int32, (128, 768), 0) + 1).astype(F32)
+    pick = jnp.where(place == slot, 1.0, 0.0).astype(BF16)
+
     def arrived(dst, sem):
         pltpu.make_async_copy(dst, dst, recv.at[sem]).wait()
 
@@ -175,6 +164,17 @@
         arrived(bb.at[n, far, quarter], S.zq + n)
         start(fx[n])
     dx = start([remote(delta_part(around(x, d)), dg.at[x, c], S.dx + d, S.dx + d, at_x(around(x, d))) for d in (2, 1, 3)])
+    for copy in token_in:
+        copy.wait()
+    mine8 = 2 * w + c
+    for n in range(4):
+        part = mm(pick, tk[:, 256 * n : 256 * n + 256]).astype(BF16)
+        pd[n, 0] = part[:, 0:128]
+        pd[n, 1] = part[:, 128:256]
+    pc[...] = mm(pick, tk[:, 1024:1536]).astype(BF16)
+    gy[y, mine8] = pd[w, c]
+    gc[mine8] = pc[...]
+
     for copy in whiten_in:
         copy.wait()
     arrive(wh)
@@ -183,7 +183,7 @@
         for d in (2, 1, 3):
             arrived(bb.at[n, far, quarter], S.fx + 4 * n + d)
         start(yf[n])
-        if n:
+        if n == 1:
             arrive(own_y[n])
             start(own_x[n])
     for n in (1, 2):
@@ -252,21 +252,23 @@
         )
 
     wx0 = whitened(0)
+    arrive(own_y[2])
+    start(own_x[2])
     arrive(dc)
     for i in range(4):
         dt[:, 256 * i : 256 * i + 256] = dg[i].reshape(256, 768).T
     wx1 = whitened(1)
     tz = [hidden(0, wx0)]
     wx2 = whitened(2)
-    tz.append(hidden(1, wx1))
-    tz.append(hidden(2, wx2))
-
     arrive(rows8)
     gy_all = start([remote(gy.at[y], gy.at[y], S.gy + d, S.gy + d, at_y(around(y, d))) for d in (1, 2, 3)])
     for d in (1, 2, 3):
         cols[d - 1].wait_recv()
         src = 2 * around(w, 4 - d) + c
         cols_c += start([remote(gc.at[src], gc.at[src], S.gr + d, S.gr + d, other)])
+
+    tz.append(hidden(1, wx1))
+    tz.append(hidden(2, wx2))
 
     spad[...] = jnp.zeros_like(spad)
     swap, rows = [], {}
@@ -296,8 +298,7 @@
     def piece(p):
         return remote(st.at[p], cg.at[from_me], S.co + p, S.co + from_me, piece_dev(p))
 
-    @pl.loop(0, 16)
-    def _(p):
+    def send_piece(p):
         here = is_me(piece_dev(p))
 
         @pl.when(here)
@@ -308,9 +309,18 @@
         def _():
             piece(p).start()
 
+    pl.loop(0, 5)(send_piece)
+
+    arrive(cols_c)
+    arrive(gy_all)
+    for i in range(4):
+        gp[i] = mm_t(gy[i].reshape(1024, 128), gc[...].reshape(1024, 512))
+    gx[...] = gp[...].astype(BF16)
     for n in parts:
         for d in (2, 1, 3):
             arrived(sx.at[n, around(x, 4 - d)], S.sl + 4 * n + d)
+    gz = start([remote(gx.at[around(x, d)], gr.at[x], S.gz + d, S.gz + d, at_x(around(x, d))) for d in (2, 1, 3)])
+
     odd = lax.rem(x, 2)
 
     @pl.when(c == x // 2)
@@ -353,12 +363,7 @@
         def _():
             copy.start()
 
-    arrive(cols_c)
-    arrive(gy_all)
-    for i in range(4):
-        gp[i] = mm_t(gy[i].reshape(1024, 128), gc[...].reshape(1024, 512))
-    gx[...] = gp[...].astype(BF16)
-    gz = start([remote(gx.at[around(x, d)], gr.at[x], S.gz + d, S.gz + d, at_x(around(x, d))) for d in (2, 1, 3)])
+    pl.loop(5, 16)(send_piece)
 
     e3 = [remote(q4, er3.at[me], S.e3 + d, S.e3 + me, exp_dev(w, c, lax.rem(me + d, 8))) for d in range(1, 8)]
 

time: 87 us -> 82 us (0.943)
  Pallas kernels: 83.5 us -> 78.7 us
    pallas_call x1, Pallas kernels: 83.5 us -> 78.7 us  [whole(): pl.pallas_call(kernel, out_shape=(jax.ShapeDtypeStruct((128, 512), F32),...]
where the time goes in v4:
time: 82 us; the launch traced here: 81.9 us
  Pallas kernels  78.7 us (96%)
  local copies, waits for them, and re-layouts  2.55 us (3%)
    pallas_call x1, Pallas kernels, whole(): pl.pallas_call(kernel, out_shape=(jax.ShapeDtypeStruct((128, 512), F32),...  78.7 us
    unnamed x3, local copies, waits for them, and re-layouts  2.55 us

profile of v4, /device:TPU:1, one launch (start us, length us, event | category | flops | bytes accessed | tf_op | source)
XLA Modules:
  0.0 81.9 jit_solution(5990070116721234205)
XLA Ops:
  0.6 78.7 %shard_map.76 = (f32[128,512]{1,0:T(8,128)S(1)}, f32[2,24,1536]{2,1,0:T(8,128)S(1)}, f32[24,768]{1,0:T(8,128)S(1)}) custom-call(bf16[768,4096]{1,0:T(8,128)(2,1)} %tokens.1, s32[8,768]{1,0:T(8,128)} %bitcast.5, bf16[2,128,4096]{2,1,0:T(8,128)(2,1)} %whiten.1, bf16[2,128,1536]{2,1,0:T(8,128)(2,1)} %deltas.1, bf16[512,768]{1,0:T(8,128)(2,1)} %basis.1), custom_call_target="tpu_custom_call" | custom-call | flops 4000000000 | bytes 20000000 | tf_op jit(solution)/shard_map/pallas_call | solution.py:430
  79.4 1.0 %copy.8 = f32[128,1,512]{2,1,0:T(1,128)} copy(f32[128,1,512]{2,0,1:T(8,128)S(1)} %bitcast.4) | data formatting | bytes 524288
  80.4 0.9 %copy.9 = f32[24,2,1536]{2,1,0:T(2,128)} copy(f32[24,2,1536]{2,0,1:T(8,128)S(1)} %bitcast.3) | data formatting | bytes 589824
  81.3 0.6 copy.11

commit v5 on v4

--- a/solution.py
+++ b/solution.py
@@ -119,7 +119,7 @@
         for n in parts
     ]
     yf = [
-        [remote(bb.at[n, far], bb.at[n, far], S.yf + 4 * n + d, S.yf + 4 * n + d, at_y(around(y, d))) for d in (2, 1, 3)]
+        [remote(bb.at[n, far], bb.at[n, far], S.yf + 4 * n + d, S.yf + 4 * n + d, at_y(around(y, d))) for d in (1, 3, 2)]
         for n in parts
     ]
     own_y = [

time: 82 us -> 82.1 us (level)
  no operation moved by 1% of the time
where the time goes in v5:
time: 82.1 us
  Pallas kernels  78.9 us (96%)
  local copies, waits for them, and re-layouts  2.55 us (3%)
    pallas_call x1, Pallas kernels, whole(): pl.pallas_call(kernel, out_shape=(jax.ShapeDtypeStruct((128, 512), F32),...  78.9 us
    unnamed x3, local copies, waits for them, and re-layouts  2.55 us

profile of v5, /device:TPU:1, one launch (start us, length us, event | category | flops | bytes accessed | tf_op | source)
XLA Modules:
  0.0 82.1 jit_solution(12468410783102662136)
XLA Ops:
  0.6 78.9 %shard_map.76 = (f32[128,512]{1,0:T(8,128)S(1)}, f32[2,24,1536]{2,1,0:T(8,128)S(1)}, f32[24,768]{1,0:T(8,128)S(1)}) custom-call(bf16[768,4096]{1,0:T(8,128)(2,1)} %tokens.1, s32[8,768]{1,0:T(8,128)} %bitcast.5, bf16[2,128,4096]{2,1,0:T(8,128)(2,1)} %whiten.1, bf16[2,128,1536]{2,1,0:T(8,128)(2,1)} %deltas.1, bf16[512,768]{1,0:T(8,128)(2,1)} %basis.1), custom_call_target="tpu_custom_call" | custom-call | flops 4000000000 | bytes 20000000 | tf_op jit(solution)/shard_map/pallas_call | solution.py:430
  79.5 1.0 %copy.8 = f32[128,1,512]{2,1,0:T(1,128)} copy(f32[128,1,512]{2,0,1:T(8,128)S(1)} %bitcast.4) | data formatting | bytes 524288
  80.5 0.9 %copy.9 = f32[24,2,1536]{2,1,0:T(2,128)} copy(f32[24,2,1536]{2,0,1:T(8,128)S(1)} %bitcast.3) | data formatting | bytes 589824
  81.4 0.6 copy.11
